TPU v7x, 512 devices: a whole 4x8x8 slice. The times are simulated.
512 devices in a mesh: section: 4 (over x), elem: 128 (over y, z, core).
Axes of the slice: x: 4, y: 8, z: 8, core: 2. Of those that a mesh axis runs over, the one named last changes fastest.
Arguments:
- interior_res: bfloat16 [3, 128, 4, 48, 100], P(None, 'elem', 'section'), may hold values from -1.5 to 1.5
- face_res: bfloat16 [3, 128, 4, 48, 4, 50], P(None, 'elem', 'section'), may hold values from -1.5 to 1.5
- trace_vals: bfloat16 [3, 128, 4, 48, 4, 50], P(None, 'elem', 'section'), may hold values from -1.5 to 1.5
- stabil: bfloat16 [128, 4, 48, 4, 25], P('elem'), may hold values from -2.5 to 2.5
- element_faces: int32 [128, 4, 48, 4], P('elem'), may hold values from 0 to 49151, as said below
- orient: int32 [128, 4, 48, 4, 10], P('elem'), may hold values from 0 to 9, as said below
- lift_matrix: bfloat16 [4, 20, 10], replicated, may hold values from -2 to 2
- face_matrix: bfloat16 [10, 10], replicated, may hold values from -2 to 2
- factors: bfloat16 [4, 128, 100, 19200], P('section', 'elem'), may hold values from -0.625 to 0.625
Outputs:
- trace_residual: float32 [3, 49152, 50], P(None, ('section', 'elem'))
- schur_product: float32 [3, 49152, 50], P(None, ('section', 'elem'))
Inputs may be any that keep to these rules, and one draw needn't show every extreme that they name: `element_faces`: every face number is named by exactly two element faces. Face f is owned by column (f // 96) % 128. For every other column, exactly 2 of a column's element faces name faces owned by that column; the rest name faces owned by the column itself. `orient`: each row of 10 numbers is one of the six node orders that the symmetries of a triangle give to the ten nodes of its degree-3 lattice.
All inputs are finite; a program needn't handle non-finite values.
Results may differ from a plain program's by a relative error of at most 0.004.
Values may be sent and summed in bfloat16 or wider, within the bound.
No kernel may reach another device: no remote copies, remote signals or barrier semaphores. Data moves between devices by JAX's collectives and lax.ppermute only.
A program may use at most 128 MiB of HBM per device.

v0:
```python
import jax
import jax.numpy as jnp
from jax import lax
from jax.sharding import PartitionSpec as P

radau_inverse = (
    (4.325579890063155, 0.33919925181580984, 0.5417705399358749),
    (-4.178718591551905, -0.32768282076106237, 0.47662355450055044),
    (-0.5028726349457868, 2.571926949855605, -0.5960392048282249),
)


def transform(sections):
    values = sections.astype(jnp.float32)
    return jnp.stack(
        [
            radau_inverse[row_index][0] * values[0]
            + radau_inverse[row_index][1] * values[1]
            + radau_inverse[row_index][2] * values[2]
            for row_index in range(3)
        ]
    ).astype(jnp.bfloat16)


def condense(
    inner_part, face_part, trace_part, stab_block, lift_matrix, face_matrix, apply_inverse
):
    highest = lax.Precision.HIGHEST
    components = inner_part.shape[0]
    number = inner_part.shape[1]
    var_count = stab_block.shape[-1]
    mode_count = inner_part.shape[2] // var_count
    lift_wide = lift_matrix.astype(jnp.float32)
    weighted = jnp.einsum(
        "ekvu,ceknu->ceknv", stab_block, trace_part, preferred_element_type=jnp.float32
    )
    lifted = jnp.einsum("kmn,ceknv->cemv", lift_wide, weighted, precision=highest)
    lifted = lifted.reshape(components, number, mode_count * var_count).astype(jnp.bfloat16)
    solved = apply_inverse(jnp.stack([inner_part, lifted], 1))
    shaped = solved.reshape(components, 2, number, mode_count, var_count)
    weighted_solve = jnp.einsum(
        "ekvu,cremu->crekmv", stab_block.astype(jnp.float32), shaped, precision=highest
    )
    coupled = jnp.einsum("kmn,crekmv->creknv", lift_wide, weighted_solve, precision=highest)
    face_term = jnp.einsum(
        "nj,cekjv->ceknv", face_matrix.astype(jnp.float32), weighted, precision=highest
    )
    return jnp.stack([face_part.astype(jnp.float32) - coupled[:, 0], face_term - coupled[:, 1]], 1)


def on_device(
    interior_res,
    face_res,
    trace_vals,
    stabil,
    element_faces,
    orient,
    lift_matrix,
    face_matrix,
    factors,
):
    elem_count = interior_res.shape[3]
    inner_size = interior_res.shape[4]
    face_size = face_res.shape[5]
    fnodes = face_matrix.shape[0]
    var_count = face_size // fnodes
    columns = lax.axis_size("elem")
    col_elems = 4 * elem_count
    third_count = elem_count // 3
    group_elems = 4 * third_count
    share_slots = elem_count // 24
    face_dev = 2 * elem_count
    col_faces = 4 * face_dev
    row_width = inner_size + 8 * face_size
    payload_width = 6 * face_size
    packed = jnp.concatenate(
        [
            interior_res.reshape(3, elem_count, inner_size),
            face_res.reshape(3, elem_count, 4 * face_size),
            trace_vals.reshape(3, elem_count, 4 * face_size),
        ],
        axis=2,
    )
    section_w = transform(packed)
    real_slot = section_w[0].reshape(1, elem_count * row_width)
    complex_slot = section_w[1:3].reshape(2, third_count, 3, row_width).transpose(2, 0, 1, 3)
    complex_slot = complex_slot.reshape(3, 2 * third_count * row_width)
    padding = jnp.zeros((3, elem_count * row_width - 2 * third_count * row_width), jnp.bfloat16)
    outgoing = jnp.concatenate(
        [real_slot, jnp.concatenate([complex_slot, padding], axis=1)], axis=0
    )
    received = lax.all_to_all(outgoing, "section", split_axis=0, concat_axis=0, tiled=True)
    section_index = lax.axis_index("section")
    stabil_col = stabil[0].reshape(4, elem_count, 4, var_count, var_count)
    factor = factors[0, 0]

    def split_rows(row_block, number):
        parts = row_block.shape[0]
        inner_part = row_block[:, :, :inner_size]
        face_part = row_block[:, :, inner_size : inner_size + 4 * face_size].reshape(
            parts, number, 4, fnodes, var_count
        )
        trace_part = row_block[:, :, inner_size + 4 * face_size :].reshape(
            parts, number, 4, fnodes, var_count
        )
        return (inner_part, face_part, trace_part)

    def real_side(rows_in):
        row_block = rows_in.reshape(1, col_elems, row_width)
        inner_part, face_part, trace_part = split_rows(row_block, col_elems)
        inverse = factor.reshape(inner_size, col_elems, inner_size)

        def apply_real(right_sides):
            return jnp.einsum(
                "iej,crej->crei", inverse, right_sides, preferred_element_type=jnp.float32
            )

        result = condense(
            inner_part,
            face_part,
            trace_part,
            stabil_col.reshape(col_elems, 4, var_count, var_count),
            lift_matrix,
            face_matrix,
            apply_real,
        )
        result = result.reshape(1, 2, 4, elem_count, 4, fnodes, var_count)
        return jnp.concatenate([result, jnp.zeros((2,) + result.shape[1:], jnp.float32)], axis=0)

    def complex_side(rows_in):
        member = section_index - 1
        row_block = rows_in[:, : 2 * third_count * row_width].reshape(4, 2, third_count, row_width)
        row_block = row_block.transpose(1, 0, 2, 3).reshape(2, group_elems, row_width)
        inner_part, face_part, trace_part = split_rows(row_block, group_elems)
        picked = lax.dynamic_index_in_dim(
            stabil_col.reshape(4, third_count, 3, 4, var_count, var_count),
            member,
            axis=2,
            keepdims=False,
        )
        picked = picked.reshape(group_elems, 4, var_count, var_count)
        real_inverse = factor[:, : group_elems * inner_size].reshape(
            inner_size, group_elems, inner_size
        )
        imag_inverse = factor[:, group_elems * inner_size : 2 * group_elems * inner_size].reshape(
            inner_size, group_elems, inner_size
        )

        def apply_complex(right_sides):
            by_real = jnp.einsum(
                "iej,crej->crei", real_inverse, right_sides, preferred_element_type=jnp.float32
            )
            by_imag = jnp.einsum(
                "iej,crej->crei", imag_inverse, right_sides, preferred_element_type=jnp.float32
            )
            return jnp.stack([by_real[0] - by_imag[1], by_imag[0] + by_real[1]])

        result = condense(
            inner_part, face_part, trace_part, picked, lift_matrix, face_matrix, apply_complex
        )
        result = result.reshape(2, 2, 4, third_count, 1, 4, fnodes, var_count)
        select = (
            (jnp.arange(3, dtype=jnp.int32) == member)
            .astype(jnp.float32)
            .reshape(1, 1, 1, 1, 3, 1, 1, 1)
        )
        spread = (result * select).reshape(2, 2, 4, elem_count, 4, fnodes, var_count)
        return jnp.concatenate([jnp.zeros((1,) + spread.shape[1:], jnp.float32), spread], axis=0)

    contrib = lax.cond(section_index == 0, real_side, complex_side, received)
    node_order = orient[0].reshape(1, 1, 4, elem_count, 4, fnodes, 1)
    oriented = jnp.take_along_axis(contrib, node_order, axis=5)
    payload = oriented.transpose(2, 3, 4, 0, 1, 5, 6).reshape(16 * elem_count, payload_width)
    face_ids = element_faces[0].reshape(-1)
    owner_col = face_ids // face_dev % columns
    owned_slot = face_ids // (face_dev * columns) * face_dev + face_ids % face_dev
    column_index = lax.axis_index("elem")
    is_local = owner_col == column_index
    local_sum = jax.ops.segment_sum(
        payload, jnp.where(is_local, owned_slot, col_faces), col_faces + 1
    )[:col_faces]
    marks = (
        (owner_col[:, None] == jnp.arange(columns, dtype=jnp.int32)[None, :])
        & jnp.logical_not(is_local)[:, None]
    ).astype(jnp.int32)
    ranking = jnp.sum(marks * (jnp.cumsum(marks, axis=0) - 1), axis=1)
    slot_index = jnp.where(is_local, columns * share_slots, owner_col * share_slots + ranking)
    outgoing_items = jax.ops.segment_sum(payload, slot_index, columns * share_slots + 1)[:-1]
    outgoing_items = outgoing_items.reshape(columns, share_slots, payload_width)
    slot_faces = jax.ops.segment_sum(owned_slot + 1, slot_index, columns * share_slots + 1)[:-1] - 1
    slot_faces = slot_faces.reshape(columns, share_slots)
    got_items, got_faces = (
        lax.all_to_all(outgoing_items, "elem", split_axis=0, concat_axis=0, tiled=True),
        lax.all_to_all(slot_faces, "elem", split_axis=0, concat_axis=0, tiled=True),
    )
    targets = jnp.where(got_faces < 0, col_faces, got_faces).reshape(-1)
    remote_sum = jax.ops.segment_sum(
        got_items.reshape(columns * share_slots, payload_width), targets, col_faces + 1
    )[:col_faces]
    combined = local_sum + remote_sum
    owned_sums = lax.psum_scatter(combined, "section", scatter_dimension=0, tiled=True)
    owned_sums = owned_sums.reshape(face_dev, 3, 2, face_size)
    return (owned_sums[:, :, 0].transpose(1, 0, 2), owned_sums[:, :, 1].transpose(1, 0, 2))


def solution(mesh):
    return jax.shard_map(
        on_device,
        mesh=mesh,
        in_specs=(
            P(None, "elem", "section", None, None),
            P(None, "elem", "section", None, None, None),
            P(None, "elem", "section", None, None, None),
            P("elem", None, None, None, None),
            P("elem", None, None, None),
            P("elem", None, None, None, None),
            P(),
            P(),
            P("section", "elem", None, None),
        ),
        out_specs=(P(None, ("section", "elem"), None), P(None, ("section", "elem"), None)),
        check_vma=False,
    )
```

profile of v0, /device:TPU:1, one launch (start us, length us, event | category | flops | bytes accessed | tf_op | source)
XLA Modules:
  0.0 508.7 jit_solution(14372178597845495554)
XLA Ops:
  7.2 1.1 reshape.497
  8.3 1.1 reshape.496
  9.3 0.9 maximum_convert_fusion
  10.4 0.3 reshape.499
  10.7 0.2 reshape_squeeze.13
  10.9 0.2 fusion.84
  11.1 0.5 broadcast.502
  11.6 0.9 reduce.8
  12.5 0.8 reshape.579
  13.3 4.8 all-to-all-start
  20.6 0.1 copy.362
  20.7 0.3 fusion.68
  21.3 0.4 fusion.72
  21.7 0.6 fusion.96
  22.3 0.6 copy-done.13
  22.9 5.8 %scatter_custom_fusion.1 = s32[257]{0:T(512)S(1)} fusion(s32[768]{0:T(1024)S(1)} %get-tuple-element.107, s32[768]{0:T(1024)S(1)} %fusion.92, s32[]{:T(128)} %constant.93.clone.1), kind=kCustom, calls=%fused_computation.144 | custom fusion | flops 768 | bytes 1032 | tf_op jit(solution)/shard_map/scatter-add | solution.py:190
  28.8 0.8 sub.62
  29.6 0.2 copy.351
  29.8 0.4 reshape.507
  30.3 0.9 copy.344
  31.2 18.3 %all-to-all-start.1 = ((s32[128,1,2]{2,1,0:T(1,128)}), s32[128,1,2]{2,1,0:T(1,128)}, u32[]{:S(2)}, u32[]{:S(2)}) async-start(s32[128,1,2]{2,1,0:T(1,128)} %bitcast.73), calls=%async_computation.1 | async-start | bytes 131072 | tf_op jit(solution)/shard_map/all_to_all | solution.py:194
  49.5 0.3 reshape.580
  49.9 89.0 %conditional.1 = (f32[3,2,4,48,4,10,5]{6,1,5,4,3,2,0:T(2,128)}) conditional(s32[]{:T(128)} %convert_element_type.90, (bf16[4,24000]{1,0:T(4,128)(2,1)S(1)}, bf16[1,4,48,4,25]{2,3,4,1,0:T(4,128)(2,1)S(1)}, s32[]{:T(128)}, bf16[4,20,10]{1,0,2:T(4,128)(2,1)S(1)}, bf16[1,1,100,19200]{3,2,1,0:T(8,128)(2,1)}, ...), branch_computations={%region_0.1_spmd, %region_1.2_spmd} | conditional | flops 49900800 | bytes 25373970 | solution.py:170
  54.7 0.4 reshape.480
  55.1 0.8 slice_convert_fusion.1
  56.0 2.3 copy.323
  58.5 3.6 copy.324
  62.1 2.8 fusion.100
  64.9 21.3 %reshape_squeeze.8 = bf16[100,192,100]{2,1,0:T(8,128)(2,1)} reshape(bf16[1,1,100,19200]{3,2,1,0:T(8,128)(2,1)} %get-tuple-element.35) | data formatting | bytes 7680000 | tf_op jit(solution)/shard_map/cond/branch_1_fun/reshape;squeeze | solution.py:111
  86.3 2.1 fusion.61
  88.6 0.8 slice_bitcast_fusion.3
  89.5 7.5 %fusion.52 = f32[1,2,192,100]{3,1,2,0:T(2,128)} fusion(bf16[100,192,100]{2,1,0:T(8,128)(2,1)} %reshape_squeeze.8, bf16[1,1,192,100]{3,1,2,0:T(2,128)(2,1)S(1)} %copy.328, bf16[1,1,192,100]{3,1,2,0:T(2,128)(2,1)S(1)} %copy.327), kind=kOutput, calls=%fused_computation.52 | convolution fusion | flops 7833600 | bytes 4070400 | tf_op jit(solution)/shard_map/cond/branch_1_fun/iej,crej->crei/dot_general | solution.py:114
  97.0 1.1 copy.330
  98.1 1.9 copy.379
  100.0 3.7 copy.380
  103.7 4.5 convolution_bitcast_fusion.2
  108.2 5.2 %fusion.43 = f32[1,2,192,4,10,5]{2,4,5,1,3,0:T(8,128)S(1)} fusion(f32[2,192,4,20,5]{3,4,2,0,1:T(8,128)S(1)} %convolution_bitcast_fusion.2, bf16[4,20,10]{1,0,2:T(4,128)(2,1)S(1)} %get-tuple-element.102), kind=kOutput, calls=%fused_computation.49 | convolution fusion | flops 18432000 | bytes 923200 | tf_op jit(solution)/shard_map/cond/branch_1_fun/kmn,crekmv->creknv/dot_general | solution.py:44
  113.4 2.7 fusion.49
  116.3 0.3 stack.45
  116.5 0.1 copy.321
  116.7 1.0 slice_subtract_fusion.2
  117.9 0.3 stack.44
  118.1 0.2 pad_maximum_fusion.3
  118.3 9.7 %copy.398 = f32[1,2,4,48,4,10,5]{6,1,5,4,3,2,0:T(2,128)} copy(f32[1,2,4,48,4,10,5]{3,2,4,6,5,1,0:T(4,128)S(1)} %pad_maximum_fusion.3) | data formatting | bytes 614400 | tf_op jit(solution)/shard_map/cond
  128.0 10.7 %concatenate.15.clone = f32[3,2,4,48,4,10,5]{6,1,5,4,3,2,0:T(2,128)} pad(f32[1,2,4,48,4,10,5]{6,1,5,4,3,2,0:T(2,128)} %copy.398, f32[]{:T(128)} %constant.60.clone), padding=0_2x0_0x0_0x0_0x0_0x0_0x0_0 | pad | bytes 1228804 | tf_op jit(solution)/shard_map/cond/branch_1_fun/concatenate | solution.py:128
  138.9 107.5 %gather_fusion = f32[7680,3,2,5]{3,2,1,0:T(2,128)} fusion(f32[3,2,4,48,4,10,5]{6,1,5,4,3,2,0:T(2,128)} %get-tuple-element.105, s32[7680]{0:T(1024)S(1)} %reshape.507), kind=kCustom, calls=%fused_computation | custom fusion | bytes 1966080 | tf_op jit(solution)/shard_map/jit(take_along_axis)/gather | solution.py:172
  246.4 42.9 %copy.393 = f32[4,48,4,10,3,2,5]{3,2,1,0,5,6,4:T(4,128)} copy(f32[4,48,4,10,3,2,5]{6,5,4,3,2,1,0:T(2,128)} %bitcast.222) | data formatting | bytes 1843200 | tf_op jit(solution)/shard_map/jit(take_along_axis)/gather | solution.py:172
  289.3 12.3 %select_bitcast_fusion = f32[4,48,4,3,2,10,5]{5,2,1,0,4,6,3:T(4,128)} fusion(f32[4,48,4,10,3,2,5]{3,2,1,0,5,6,4:T(4,128)} %copy.393, pred[4,48,4,10]{3,2,1,0:T(4,128)(4,1)S(1)} %copy-done.8), kind=kLoop, calls=%fused_computation.68 | loop fusion | flops 230400 | bytes 1850880 | tf_op jit(solution)/shard_map/jit(take_along_axis)/select_n | solution.py:172
  301.6 41.2 %copy.354 = f32[4,48,4,3,2,10,5]{2,1,0,6,5,4,3:T(8,128)} copy(f32[4,48,4,3,2,10,5]{5,2,1,0,4,6,3:T(4,128)} %select_bitcast_fusion) | data formatting | bytes 1843200 | tf_op jit(solution)/shard_map/jit(take_along_axis)/select_n | solution.py:172
  342.9 25.8 %reshape.533 = f32[768,300]{0,1:T(8,128)S(1)} reshape(f32[4,48,4,3,2,10,5]{2,1,0,6,5,4,3:T(8,128)} %copy.354) | data formatting | bytes 1843200 | tf_op jit(solution)/shard_map/reshape | solution.py:173
  368.7 0.4 copy.355
  369.1 6.8 %scatter_custom_fusion.2 = f32[257,300]{1,0:T(8,128)S(1)} fusion(s32[768]{0:T(1024)} %copy-done.13, f32[768,300]{1,0:T(8,128)S(1)} %copy.355, f32[]{:T(128)} %constant.90.clone.1), kind=kCustom, calls=%fused_computation.89 | custom fusion | flops 230400 | bytes 308912 | tf_op jit(solution)/shard_map/scatter-add | solution.py:188
  375.9 1.0 reshape.502
  376.9 13.7 %all-to-all-start.2 = ((f32[128,2,300]{2,1,0:T(2,128)}), f32[128,2,300]{2,1,0:T(2,128)S(1)}, u32[]{:S(2)}, u32[]{:S(2)}) async-start(f32[128,2,300]{2,1,0:T(2,128)} %reshape.502), calls=%async_computation.2 | async-start | bytes 786432 | tf_op jit(solution)/shard_map/all_to_all | solution.py:193
  390.7 0.5 broadcast.499
  391.2 1.6 reduce.7
  393.0 6.8 %scatter_custom_fusion = f32[385,300]{1,0:T(8,128)S(1)} fusion(s32[768]{0:T(1024)} %get-tuple-element.106, f32[768,300]{1,0:T(8,128)S(1)} %copy.355, f32[]{:T(128)} %constant.90.clone.1), kind=kCustom, calls=%fused_computation.83 | custom fusion | flops 230400 | bytes 462512 | tf_op jit(solution)/shard_map/scatter-add | solution.py:179
  399.8 7.6 %all-to-all-done.2 = f32[128,2,300]{2,1,0:T(2,128)S(1)} async-done(((f32[128,2,300]{2,1,0:T(2,128)}), f32[128,2,300]{2,1,0:T(2,128)S(1)}, u32[]{:S(2)}, u32[]{:S(2)}) %all-to-all-start.2) | async-done | bytes 307232 | tf_op jit(solution)/shard_map/all_to_all | solution.py:193
  407.4 0.3 reshape.541
  407.7 2.2 scatter_custom_fusion.3
  409.9 0.9 slice_add_fusion.1
  410.8 88.9 %reduce-scatter.2.cloned.1.call-done = f32[96,300]{1,0:T(8,128)} async-done(((f32[384,300]{1,0:T(8,128)}), f32[96,300]{1,0:T(8,128)}) %reduce-scatter.2.cloned.1.call-update) | async-done | bytes 115216 | tf_op jit(solution)/shard_map/reduce_scatter | solution.py:201
  499.7 1.0 copy.368
  500.8 0.7 slice_bitcast_fusion.4
  (73 shorter events, 4.0 us)
Async XLA Ops:
  7.2 11.0 %copy-start.11 = (s32[1,4,48,4]{2,3,1,0:T(4,128)S(1)}, s32[1,4,48,4]{2,3,1,0:T(4,128)}, u32[]{:S(2)}) copy-start(s32[1,4,48,4]{2,3,1,0:T(4,128)} %param.15) | copy-start | bytes 9220
  10.7 18.8 %copy-start.9 = (s32[1,4,48,4,10]{2,3,4,1,0:T(4,128)S(1)}, s32[1,4,48,4,10]{2,3,4,1,0:T(4,128)}, u32[]{:S(2)}) copy-start(s32[1,4,48,4,10]{2,3,4,1,0:T(4,128)} %param.16) | copy-start | bytes 92164
  13.3 17.8 %all-to-all-start = ((bf16[4,2,12000]{2,1,0:T(2,128)(2,1)}), bf16[4,2,12000]{2,1,0:T(2,128)(2,1)S(1)}, u32[]{:S(2)}, u32[]{:S(2)}) async-start(bf16[4,2,12000]{2,1,0:T(2,128)(2,1)} %reshape.579), calls=%async_computation | async-start | bytes 385024 | tf_op jit(solution)/shard_map/all_to_all | solution.py:92
  19.4 30.5 %copy-start.6 = (bf16[4,20,10]{1,0,2:T(4,128)(2,1)S(1)}, bf16[4,20,10]{1,0,2:T(4,128)(2,1)}, u32[]{:S(2)}) copy-start(bf16[4,20,10]{1,0,2:T(4,128)(2,1)} %param.17) | copy-start | bytes 4804
  19.4 30.5 %copy-start.7 = (bf16[1,4,48,4,25]{2,3,4,1,0:T(4,128)(2,1)S(1)}, bf16[1,4,48,4,25]{2,3,4,1,0:T(4,128)(2,1)}, u32[]{:S(2)}) copy-start(bf16[1,4,48,4,25]{2,3,4,1,0:T(4,128)(2,1)} %param.14) | copy-start | bytes 115204
  19.4 30.5 %copy-start.12 = (bf16[10,10]{1,0:T(8,128)(2,1)S(1)}, bf16[10,10]{1,0:T(8,128)(2,1)}, u32[]{:S(2)}) copy-start(bf16[10,10]{1,0:T(8,128)(2,1)} %param.18) | copy-start | bytes 604
  22.3 0.6 copy-start.13
  31.2 345.7 %all-to-all-start.1 = ((s32[128,1,2]{2,1,0:T(1,128)}), s32[128,1,2]{2,1,0:T(1,128)}, u32[]{:S(2)}, u32[]{:S(2)}) async-start(s32[128,1,2]{2,1,0:T(1,128)} %bitcast.73), calls=%async_computation.1 | async-start | bytes 131072 | tf_op jit(solution)/shard_map/all_to_all | solution.py:194
  55.1 3.5 copy-start.2
  108.2 8.3 %copy-start.3 = (f32[1,192,200]{2,1,0:T(8,128)S(1)}, f32[1,192,200]{2,1,0:T(8,128)}, u32[]{:S(2)}) copy-start(f32[1,192,200]{2,1,0:T(8,128)} %get-tuple-element.120) | copy-start | bytes 460804 | tf_op jit(solution)/shard_map/cond
  113.4 2.7 copy-start.1
  246.4 42.9 %copy-start.8 = (pred[4,48,4,10]{3,2,1,0:T(4,128)(4,1)S(1)}, pred[4,48,4,10]{3,2,1,0:T(4,128)(4,1)}, u32[]{:S(2)}) copy-start(pred[4,48,4,10]{3,2,1,0:T(4,128)(4,1)} %copy.344) | copy-start | bytes 23044
  376.9 30.5 %all-to-all-start.2 = ((f32[128,2,300]{2,1,0:T(2,128)}), f32[128,2,300]{2,1,0:T(2,128)S(1)}, u32[]{:S(2)}, u32[]{:S(2)}) async-start(f32[128,2,300]{2,1,0:T(2,128)} %reshape.502), calls=%async_computation.2 | async-start | bytes 786432 | tf_op jit(solution)/shard_map/all_to_all | solution.py:193
  390.6 109.1 %reduce-scatter.2.cloned.1.call-start = ((), (), s32[]{:S(2)}) async-start(), calls=%async_computation.4 | async-start | bytes 737280 | tf_op jit(solution)/shard_map/reduce_scatter | solution.py:201
Sparse Core Ops, SparseCore 0:
  410.9 88.7 reduce-scatter.1
where the time goes:
time: 518 us; the launch traced here: 509 us
  local copies, waits for them, and re-layouts  288 us (56%)
  waiting for transfers between devices  96.5 us (19%)
  other arithmetic  42.2 us (8%)
  starting transfers between devices  36.9 us (7%)
  matrix products  24.8 us (5%)
  between operations  14.9 us (3%)
    gather x4, local copies, waits for them, and re-layouts, on_device(): oriented = jnp.take_along_axis(contrib, node_order, axis=5)  151 us
    reduce_scatter x1, waiting for transfers between devices, on_device(): lax.psum_scatter(combined, 'section', scatter_dimension=0, tiled=True)  88.9 us
    select_n x1, local copies, waits for them, and re-layouts, on_device(): oriented = jnp.take_along_axis(contrib, node_order, axis=5)  41.2 us
    reshape x2, local copies, waits for them, and re-layouts, on_device(): oriented.transpose(2, 3, 4, 0, 1, 5, 6)  26.2 us
    another operation x1, local copies, waits for them, and re-layouts, real_side(): inverse = factor.reshape(inner_size, col_elems, inner_size)  21.3 us
    all_to_all x1, starting transfers between devices, on_device(): lax.all_to_all(slot_faces, 'elem', split_axis=0, concat_axis=0, tiled=True)  18.3 us
    all_to_all x1, starting transfers between devices, on_device(): lax.all_to_all(outgoing_items, 'elem', split_axis=0, concat_axis=0, tiled...  13.7 us
    select_n x1, other arithmetic, on_device(): oriented = jnp.take_along_axis(contrib, node_order, axis=5)  12.3 us
  transfers between devices with their start and end apart: 4, of which 2 were waited for; matrix products, arithmetic and copies ran while one was open for 68% of the time, Pallas kernels for 0%

commit v1 on v0

v1 whole, which is shorter than its diff:
```python
import jax
import jax.numpy as jnp
import numpy as np
from jax import lax
from jax.experimental import pallas as pl
from jax.experimental.pallas import tpu as pltpu
from jax.sharding import PartitionSpec as P

TI = (
    (4.325579890063155, 0.33919925181580984, 0.5417705399358749),
    (-4.178718591551905, -0.32768282076106237, 0.47662355450055044),
    (-0.5028726349457868, 2.571926949855605, -0.5960392048282249),
)
VARS, MODES, FN, NI, NF = 5, 20, 10, 100, 50
ELEMS, COLE, GRP, COLS, FDEV = 48, 192, 64, 128, 96
SLOTS = 4 * FDEV
W = 512
UW = VARS * W
CH = 3200
BF, F32, I32 = jnp.bfloat16, jnp.float32, jnp.int32
VMEM = pl.BlockSpec(memory_space=pltpu.VMEM)


def code_tables():
    cols = np.full((16, UW), -1, np.int32)
    for u in range(VARS):
        for k in range(4):
            for o in range(2):
                for n in range(FN):
                    for v in range(VARS):
                        lane = u * W + k * 128 + o * 64 + n * VARS + v
                        cols[0, lane] = k * 25 + v * 5 + u
                        cols[1, lane] = k * 5 + u
                        cols[2, lane] = o * FN + n
                        cols[3, lane] = k * FN + n
                        cols[4, lane] = u * 2 + o
                        cols[5, lane] = v if o == 0 else -1
                        cols[7, lane] = o
                        cols[8, lane] = k * NF + n * VARS + v if o == 0 else -1
    lanes = np.arange(UW) % 128
    cols[6] = np.where(cols[0] < 0, lanes, (lanes // 64) * 64 + (lanes % 64) % 5)
    rows = np.full((256, 128), -1, np.int32)
    for i in range(200):
        rows[i, 0] = (i // 50) * 5 + i % 5
        rows[i, 1] = (i % 50) // 5
    for x in range(2):
        for i in range(NI):
            rows[x * 128 + i, 2] = (i % 5) * 2 + x
            rows[x * 128 + i, 3] = i // 5
            rows[x * 128 + i, 4] = i % 5
    lane = np.arange(CH)
    tiles = np.zeros((8, CH), np.int32)
    tiles[0] = lane % NI
    tiles[1] = lane // NI
    return cols, rows, tiles


COL_CODES, ROW_CODES, TILE_CODES = code_tables()


def dot(a, b):
    return lax.dot_general(a, b, (((1,), (0,)), ((), ())), preferred_element_type=F32)


def dot_t(a, b):
    return lax.dot_general(a, b, (((1,), (1,)), ((), ())), preferred_element_type=F32)


def iota(shape, dim):
    return lax.broadcasted_iota(I32, shape, dim)


def onehot(cond):
    return jnp.where(cond, 1.0, 0.0).astype(BF)


def split(x):
    hi = x.astype(BF)
    return hi, (x - hi.astype(F32)).astype(BF)


def pack_kernel(inner_ref, face_ref, trace_ref, out_ref):
    out_ref[...] = jnp.zeros(out_ref.shape, BF)
    row = iota((ELEMS, ELEMS), 0)
    pick = onehot(iota((ELEMS, ELEMS), 1) == 3 * (row & 15) + (row >> 4))
    for ref, lane, width in ((inner_ref, 0, NI), (face_ref, 128, 4 * NF), (trace_ref, 384, 4 * NF)):
        vals = [ref[t].astype(F32) for t in range(3)]
        for g in range(3):
            mixed = (TI[g][0] * vals[0] + TI[g][1] * vals[1] + TI[g][2] * vals[2]).astype(BF)
            if g == 0:
                out_ref[0, :, lane : lane + width] = mixed
            else:
                moved = dot(pick, mixed).astype(BF)
                for t in range(3):
                    out_ref[1 + t, 16 * (g - 1) : 16 * g, lane : lane + width] = moved[
                        16 * t : 16 * t + 16
                    ]


def prep_kernel(
    where_ref, stab_ref, orient_ref, faces_ref, lift_ref, mass_ref, cols_ref, rows_ref, tiles_ref,
    s_ref, gg_ref, qq_ref, lm_ref, p0_ref, idx_ref, ab_ref, out_hot_ref, loc_hot_ref, tile_ref, bd_ref,
):
    section = where_ref[0]
    column = where_ref[1]
    row = iota((COLE, COLE), 0)
    third = section - 1
    target = jnp.where(
        section == 0, row, jnp.where(row < GRP, 48 * (row >> 4) + 3 * (row & 15) + third, -1)
    )
    pick = onehot(target == iota((COLE, COLE), 1))
    stab = dot(pick, stab_ref[...]).astype(BF)
    orient = dot(pick, orient_ref[...]).astype(BF)
    spread_kn = onehot(iota((40, UW), 0) == cols_ref[3:4, :])
    for u in range(VARS):
        cut = slice(u * W, (u + 1) * W)
        expand = onehot(iota((100, W), 0) == cols_ref[0:1, cut])
        s_ref[:, cut] = dot(stab, expand)
    nodes = dot(orient, spread_kn[:, :W])
    idx_ref[...] = (VARS * nodes).astype(I32) + cols_ref[6:7, :W]
    pick_j = onehot(rows_ref[:, 1:2] == iota((256, FN), 1))
    mass = dot_t(pick_j, mass_ref[...]).astype(BF)
    pick_m = onehot(rows_ref[:, 3:4] == iota((256, MODES), 1))
    lift = dot(pick_m, lift_ref[...]).astype(BF)
    for u in range(VARS):
        cut = slice(u * W, (u + 1) * W)
        plain = onehot(iota((FN, W), 0) == cols_ref[2:3, cut])
        massed = onehot(iota((FN, W), 0) + FN == cols_ref[2:3, cut])
        full = dot(pick_j, plain) + dot(mass, massed)
        gg_ref[:, cut] = jnp.where(rows_ref[:, 0:1] == cols_ref[1:2, cut], full, 0.0).astype(BF)
        full = dot(lift, spread_kn[:, cut])
        qq_ref[:, cut] = jnp.where(rows_ref[:, 2:3] == cols_ref[4:5, cut], full, 0.0).astype(BF)
        if u == 0:
            keep = rows_ref[:128, 4:5] == cols_ref[5:6, cut]
            keep = keep & (cols_ref[5:6, cut] >= 0)
            lm_ref[...] = jnp.where(keep, full[:128], 0.0).astype(BF)
    p0_ref[...] = onehot(iota((256, W), 0) == cols_ref[8:9, :W])
    tile_ref[...] = onehot(iota((128, CH), 0) == tiles_ref[0:1, :])
    bd_ref[...] = jnp.where(iota((32, CH), 0) == tiles_ref[1:2, :], 1.0, 0.0)
    face = faces_ref[...]
    block = ((face >> 5) * 43691) >> 17
    owner = block & (COLS - 1)
    slot = (block >> 7) * FDEV + face - block * FDEV
    away = owner != column
    lane = iota((COLE, 16), 1)
    codes = jnp.zeros((COLE, 16), I32)
    fields = (jnp.where(away, owner + 1, 0), jnp.where(away, 0, 1), slot >> 5, slot & 31)
    for f, field in enumerate(fields):
        for k in range(4):
            codes = jnp.where(lane == 4 * f + k, field[:, k : k + 1], codes)
    codes = dot(pick, codes.astype(F32).astype(BF))
    ab_ref[...] = codes
    turned = dot_t(onehot(iota((16, 16), 0) == iota((16, 16), 1)), codes.astype(BF))
    before = onehot(iota((COLE, COLE), 0) < iota((COLE, COLE), 1))
    count = jnp.zeros((COLS, 1), F32)
    own_iota = iota((COLS, COLE), 0) + 1
    for k in range(4):
        own = turned[k : k + 1, :].astype(I32)
        hot = own_iota == own
        hot_f = jnp.where(hot, 1.0, 0.0)
        rank = dot(hot_f.astype(BF), before) + count
        count = count + jnp.sum(hot_f, axis=1, keepdims=True)
        rank = jnp.sum(jnp.where(hot, rank, 0.0), axis=0, keepdims=True).astype(I32)
        key = jnp.where(own > 0, 2 * (own - 1) + rank, -1)
        out_hot_ref[k] = onehot(iota((2 * COLS, COLE), 0) == key)
        slots = (32.0 * turned[8 + k : 9 + k, :] + turned[12 + k : 13 + k, :]).astype(I32)
        slots = jnp.where(turned[4 + k : 5 + k, :] > 0.5, slots, -1)
        loc_hot_ref[k] = onehot(iota((SLOTS, COLE), 0) == slots)


def main_kernel(
    where_ref, rec_ref, s_ref, gg_ref, qq_ref, lm_ref, p0_ref, idx_ref, ab_ref, hot_ref, tile_ref,
    bd_ref, cols_ref, factor_ref, pay_ref, con_ref, fac_ref, sol_ref, sem_ref,
):
    section = where_ref[0]

    def fetch(c):
        cut = pl.ds(c * CH, CH)
        return pltpu.make_async_copy(factor_ref.at[:, cut], fac_ref.at[:, cut], sem_ref.at[c])

    def finish(x_in, number, parts, solve):
        total = number * parts

        def s_of(u):
            s = s_ref[:number, u * W : (u + 1) * W]
            return jnp.concatenate([s] * parts, axis=0) if parts > 1 else s

        trace = x_in[:, 384:640]
        value = jnp.zeros((total, W), F32)
        for u in range(VARS):
            value = value + s_of(u) * dot(trace, gg_ref[:, u * W : (u + 1) * W])
        hi, lo = split(value)
        lifted = (dot_t(hi, lm_ref[...]) + dot_t(lo, lm_ref[...])).astype(BF)
        sol_ref[...] = jnp.zeros(sol_ref.shape, F32)
        solve(x_in[:, :128], lifted)
        hi, lo = split(sol_ref[:total, :])
        base = jnp.where(cols_ref[7:8, :W] == 1, value, 0.0) + dot(x_in[:, 128:384], p0_ref[...])
        for u in range(VARS):
            cut = slice(u * W, (u + 1) * W)
            base = base - s_of(u) * (dot(hi, qq_ref[:, cut]) + dot(lo, qq_ref[:, cut]))
        con_ref[...] = jnp.zeros(con_ref.shape, BF)
        lane = iota((number, 128), 1)
        pay = [jnp.zeros((2 * COLS, 128), F32) for _ in range(parts)]
        for k in range(4):
            index = idx_ref[:number, 128 * k : 128 * k + 128]
            for c in range(parts):
                piece = base[c * number : (c + 1) * number, 128 * k : 128 * k + 128]
                piece = jnp.take_along_axis(piece, index, axis=1, mode="promise_in_bounds")
                if c == 0:
                    piece = jnp.where(lane == NF, ab_ref[:number, 8 + k : 9 + k], piece)
                    piece = jnp.where(lane == NF + 1, ab_ref[:number, 12 + k : 13 + k], piece)
                piece = piece.astype(BF)
                con_ref[k, :number, 128 * c : 128 * c + 128] = piece
                pay[c] = pay[c] + dot(hot_ref[k, :, :number], piece)
        for c in range(2):
            pay_ref[:, 128 * c : 128 * c + 128] = (
                pay[c].astype(BF) if c < parts else jnp.zeros((2 * COLS, 128), BF)
            )

    @pl.when(section == 0)
    def _():
        for c in range(6):
            fetch(c).start()
        x_in = jnp.concatenate([rec_ref[s] for s in range(4)], axis=0)

        def solve(inner, lifted):
            keep = jnp.concatenate([bd_ref[...]] * 2, axis=0)
            for c in range(6):
                cut = slice(32 * c, 32 * c + 32)
                x = jnp.concatenate([inner[cut], lifted[cut]], axis=0)
                x = (dot(x, tile_ref[...]) * keep).astype(BF)
                fetch(c).wait()
                y = dot_t(x, fac_ref[:, c * CH : (c + 1) * CH])
                sol_ref[cut, 0:NI] = y[:32]
                sol_ref[cut, 128 : 128 + NI] = y[32:]

        finish(x_in, COLE, 1, solve)

    @pl.when(section != 0)
    def _():
        for c in range(4):
            fetch(c).start()
        x_in = jnp.concatenate(
            [rec_ref[s, 16 * g : 16 * g + 16] for g in range(2) for s in range(4)], axis=0
        )

        def solve(inner, lifted):
            keep = jnp.concatenate([bd_ref[...]] * 4, axis=0)
            waited = []
            for c in range(2):
                re = slice(32 * c, 32 * c + 32)
                im = slice(GRP + 32 * c, GRP + 32 * c + 32)
                x = jnp.concatenate([inner[re], lifted[re], inner[im], lifted[im]], axis=0)
                x = (dot(x, tile_ref[...]) * keep).astype(BF)
                fetch(c).wait()
                a = dot_t(x, fac_ref[:, c * CH : (c + 1) * CH])
                fetch(2 + c).wait()
                b = dot_t(x, fac_ref[:, (2 + c) * CH : (3 + c) * CH])
                real = a[:64] - b[64:]
                imag = b[:64] + a[64:]
                sol_ref[re, 0:NI] = real[:32]
                sol_ref[re, 128 : 128 + NI] = real[32:]
                sol_ref[im, 0:NI] = imag[:32]
                sol_ref[im, 128 : 128 + NI] = imag[32:]

        finish(x_in, GRP, 2, solve)


def local_kernel(hot_ref, con_ref, out_ref):
    total = dot(hot_ref[0], con_ref[0])
    for k in range(1, 4):
        total = total + dot(hot_ref[k], con_ref[k])
    out_ref[...] = total


def place_kernel(got_ref, loc_ref, out_ref):
    got = got_ref[...]
    lane = iota((8, 128), 1)
    weights = jnp.where(lane == NF, 32.0, jnp.where(lane == NF + 1, 1.0, 0.0)).astype(BF)
    slot = dot_t(weights, got[:, :128])[0:1].astype(I32)
    hot = onehot(iota((SLOTS, 2 * COLS), 0) == slot)
    total = loc_ref[...] + dot(hot, got)
    for s in range(4):
        out_ref[s] = total[FDEV * s : FDEV * s + FDEV].astype(BF)


def sum_kernel(got_ref, res_ref, schur_ref):
    sums = [
        got_ref[0, :, :128].astype(F32),
        got_ref[1, :, :128].astype(F32)
        + got_ref[2, :, :128].astype(F32)
        + got_ref[3, :, :128].astype(F32),
        got_ref[1, :, 128:].astype(F32)
        + got_ref[2, :, 128:].astype(F32)
        + got_ref[3, :, 128:].astype(F32),
    ]
    for g in range(3):
        res_ref[g] = sums[g][:, :NF]
        schur_ref[g] = pltpu.roll(sums[g], 64, 1)[:, :NF]


def shape(dims, kind):
    return jax.ShapeDtypeStruct(dims, kind)


def cost(flops, nbytes):
    return pl.CostEstimate(flops=flops, bytes_accessed=nbytes, transcendentals=0)


def on_device(
    interior_res, face_res, trace_vals, stabil, element_faces, orient, lift_matrix, face_matrix, factors
):
    smem = pl.BlockSpec(memory_space=pltpu.SMEM)
    where = jnp.stack([lax.axis_index("section"), lax.axis_index("elem")]).astype(I32)
    params = pltpu.CompilerParams(vmem_limit_bytes=56 * 2**20)
    send = pl.pallas_call(
        pack_kernel,
        name="pack",
        out_shape=shape((4, ELEMS, 640), BF),
        in_specs=[VMEM] * 3,
        out_specs=VMEM,
        cost_estimate=cost(10**8, 10**6),
    )(
        interior_res.reshape(3, ELEMS, NI),
        face_res.reshape(3, ELEMS, 4 * NF),
        trace_vals.reshape(3, ELEMS, 4 * NF),
    )
    received = lax.all_to_all(send, "section", split_axis=0, concat_axis=0, tiled=True)
    cols, rows, tiles = jnp.asarray(COL_CODES), jnp.asarray(ROW_CODES), jnp.asarray(TILE_CODES)
    s_all, gg, qq, lm, p0, idx, ab, out_hot, loc_hot, tile, bd = pl.pallas_call(
        prep_kernel,
        name="prep",
        out_shape=(
            shape((COLE, UW), F32),
            shape((256, UW), BF),
            shape((256, UW), BF),
            shape((128, W), BF),
            shape((256, W), BF),
            shape((COLE, W), I32),
            shape((COLE, 16), F32),
            shape((4, 2 * COLS, COLE), BF),
            shape((4, SLOTS, COLE), BF),
            shape((128, CH), BF),
            shape((32, CH), F32),
        ),
        in_specs=[smem] + [VMEM] * 8,
        out_specs=[VMEM] * 11,
        compiler_params=params,
        cost_estimate=cost(10**9, 8 * 10**6),
    )(
        where,
        stabil.reshape(COLE, 100),
        orient.reshape(COLE, 40).astype(BF),
        element_faces.reshape(COLE, 4),
        lift_matrix.transpose(1, 0, 2).reshape(MODES, 4 * FN),
        face_matrix,
        cols,
        rows,
        tiles,
    )
    payload, contrib = pl.pallas_call(
        main_kernel,
        name="condense",
        out_shape=(shape((2 * COLS, 256), BF), shape((4, COLE, 256), BF)),
        in_specs=[smem] + [VMEM] * 12 + [pl.BlockSpec(memory_space=pl.ANY)],
        out_specs=[VMEM] * 2,
        scratch_shapes=[
            pltpu.VMEM((NI, COLE * NI), BF),
            pltpu.VMEM((COLE, 256), F32),
            pltpu.SemaphoreType.DMA((6,)),
        ],
        compiler_params=params,
        cost_estimate=cost(10**9, 8 * 10**6),
    )(
        where, received, s_all, gg, qq, lm, p0, idx, ab, out_hot, tile, bd, cols,
        factors.reshape(NI, COLE * NI),
    )
    got = lax.all_to_all(
        payload.reshape(COLS, 2, 256), "elem", split_axis=0, concat_axis=0, tiled=True
    )
    local = pl.pallas_call(
        local_kernel,
        name="local",
        out_shape=shape((SLOTS, 256), F32),
        in_specs=[VMEM] * 2,
        out_specs=VMEM,
        cost_estimate=cost(3 * 10**8, 2 * 10**6),
    )(loc_hot, contrib)
    partial = pl.pallas_call(
        place_kernel,
        name="place",
        out_shape=shape((4, FDEV, 256), BF),
        in_specs=[VMEM] * 2,
        out_specs=VMEM,
        cost_estimate=cost(10**8, 10**6),
    )(got.reshape(2 * COLS, 256), local)
    parts = lax.all_to_all(partial, "section", split_axis=0, concat_axis=0, tiled=True)
    return tuple(
        pl.pallas_call(
            sum_kernel,
            name="total",
            out_shape=(shape((3, FDEV, NF), F32), shape((3, FDEV, NF), F32)),
            in_specs=[VMEM],
            out_specs=[VMEM] * 2,
            cost_estimate=cost(10**6, 10**6),
        )(parts)
    )


def solution(mesh):
    return jax.shard_map(
        on_device,
        mesh=mesh,
        in_specs=(
            P(None, "elem", "section", None, None),
            P(None, "elem", "section", None, None, None),
            P(None, "elem", "section", None, None, None),
            P("elem", None, None, None, None),
            P("elem", None, None, None),
            P("elem", None, None, None, None),
            P(),
            P(),
            P("section", "elem", None, None),
        ),
        out_specs=(P(None, ("section", "elem"), None), P(None, ("section", "elem"), None)),
        check_vma=False,
    )
```

time: 518 us -> 83.9 us (0.16); the launches traced: 509 us -> 83.1 us
  local copies, waits for them, and re-layouts: 288 us -> 15.3 us
  waiting for transfers between devices: 96.5 us -> 9.92 us
  other arithmetic: 42.2 us -> 1.51 us
  matrix products: 24.8 us -> 0 us
  Pallas kernels: 0 us -> 23.7 us
  between operations: 14.9 us -> 0.7 us
  starting transfers between devices: 36.9 us -> 22.7 us
  blocking collectives: 0 us -> 9.23 us
    gather x4 -> x0, local copies, waits for them, and re-layouts: 151 us -> none  [on_device(): oriented = jnp.take_along_axis(contrib, node_order, axis=5)]
    reduce_scatter x1 -> x0, waiting for transfers between devices: 88.9 us -> none  [on_device(): lax.psum_scatter(combined, 'section', scatter_dimension=0, tiled=True)]
    select_n x2 -> x0, local copies, waits for them, and re-layouts: 41.4 us -> none  [the longest x1 41.2 us: on_device(): oriented = jnp.take_along_axis(contrib, node_order, axis=5)]
    another operation x15 -> x0, local copies, waits for them, and re-layouts: 34.8 us -> none  [the longest x1 21.3 us: real_side(): inverse = factor.reshape(inner_size, col_elems, inner_size)]
    dot_general x6 -> x0, matrix products: 24.8 us -> none  [the longest x1 7.49 us: apply_real(): jnp.einsum('iej,crej->crei', inverse, right_sides, preferred_element_type...]
    pallas_call x0 -> x6, Pallas kernels: none -> 23.7 us  [the longest x1 9.48 us: on_device(): pl.pallas_call(main_kernel, name='condense', out_shape=(shape((2 * COLS,...]
    reshape x9 -> x8, local copies, waits for them, and re-layouts: 30.2 us -> 8.09 us  [the longest x1 1.7 us: on_device(): face_res.reshape(3, ELEMS, 4 * NF)]
    scatter-add x4 -> x0, other arithmetic: 21.7 us -> none  [the longest x1 6.83 us: on_device(): jax.ops.segment_sum(payload, jnp.where(is_local, owned_slot, col_faces),...]
  transfers between devices with their start and end apart: 4 -> 2, of which waited for: 2 -> 1; matrix products, arithmetic and copies ran while one was open for 68% -> 9% of each run, Pallas kernels for 0% -> 10%
where the time goes in v1:
time: 83.9 us; the launch traced here: 83.1 us
  Pallas kernels  23.7 us (28%)
  starting transfers between devices  22.7 us (27%)
  local copies, waits for them, and re-layouts  15.3 us (18%)
  waiting for transfers between devices  9.92 us (12%)
  blocking collectives  9.23 us (11%)
  other arithmetic  1.51 us (2%)
    all_to_all x1, starting transfers between devices, on_device(): lax.all_to_all(payload.reshape(COLS, 2, 256), 'elem', split_axis=0, conca...  17.9 us
    all_to_all x1, waiting for transfers between devices, on_device(): lax.all_to_all(payload.reshape(COLS, 2, 256), 'elem', split_axis=0, conca...  9.92 us
    pallas_call x1, Pallas kernels, on_device(): pl.pallas_call(main_kernel, name='condense', out_shape=(shape((2 * COLS,...  9.48 us
    all_to_all x1, blocking collectives, on_device(): lax.all_to_all(partial, 'section', split_axis=0, concat_axis=0, tiled=True)  9.23 us
    pallas_call x1, Pallas kernels, on_device(): pl.pallas_call(prep_kernel, name='prep', out_shape=(shape((COLE, UW), F32...  6.25 us
    all_to_all x1, starting transfers between devices, on_device(): lax.all_to_all(send, 'section', split_axis=0, concat_axis=0, tiled=True)  4.83 us
    pallas_call x2, local copies, waits for them, and re-layouts, on_device(): pl.pallas_call(sum_kernel, name='total', out_shape=(shape((3, FDEV, NF),...  3.31 us
    unnamed x4, local copies, waits for them, and re-layouts  3.09 us
  transfers between devices with their start and end apart: 2, of which 1 were waited for; matrix products, arithmetic and copies ran while one was open for 9% of the time, Pallas kernels for 10%

profile of v1, /device:TPU:1, one launch (start us, length us, event | category | flops | bytes accessed | tf_op | source)
XLA Modules:
  0.0 83.1 jit_solution(13992284745643734970)
XLA Ops:
  0.6 1.7 %reshape.34.face_ref = bf16[3,48,200]{2,1,0:T(8,128)(2,1)} reshape(bf16[3,1,1,48,4,50]{5,4,3,2,1,0:T(4,128)(2,1)} %param.13) | data formatting | bytes 115200 | tf_op jit(solution)/shard_map/reshape | solution.py:325
  2.3 1.7 %reshape.35.trace_ref = bf16[3,48,200]{2,1,0:T(8,128)(2,1)} reshape(bf16[3,1,1,48,4,50]{5,4,3,2,1,0:T(4,128)(2,1)} %param.14) | data formatting | bytes 115200 | tf_op jit(solution)/shard_map/reshape | solution.py:326
  4.0 1.9 %pack.1 = bf16[4,48,640]{2,1,0:T(8,128)(2,1)} custom-call(bf16[3,48,100]{2,1,0:T(8,128)(2,1)} %bitcast.12, bf16[3,48,200]{2,1,0:T(8,128)(2,1)} %reshape.34.face_ref, bf16[3,48,200]{2,1,0:T(8,128)(2,1)} %reshape.35.trace_ref), custom_call_target="tpu_custom_call" | custom-call | flops 100000000 | bytes 1000000 | tf_op jit(solution)/shard_map/pack/pallas_call | solution.py:316
  5.9 4.8 %all-to-all-start = ((bf16[4,48,640]{2,1,0:T(8,128)(2,1)}), bf16[4,48,640]{2,1,0:T(8,128)(2,1)S(1)}, u32[]{:S(2)}, u32[]{:S(2)}) async-start(bf16[4,48,640]{2,1,0:T(8,128)(2,1)} %pack.1), calls=%async_computation | async-start | bytes 491520 | tf_op jit(solution)/shard_map/all_to_all | solution.py:328
  10.7 0.8 copy.29
  11.6 0.7 reshape.42.lift_ref
  12.2 0.9 %convert_element_type.5 = bf16[1,4,48,4,10]{2,3,4,1,0:T(4,128)(2,1)S(1)} convert(s32[1,4,48,4,10]{2,3,4,1,0:T(4,128)} %param.17) | non-fusion elementwise | flops 7680 | bytes 46080 | tf_op jit(solution)/shard_map/convert_element_type | solution.py:353
  13.2 0.1 convert_element_type.6
  13.3 0.7 copy.25.orient_ref
  14.0 1.4 %copy.22 = s32[1,4,48,4]{3,2,1,0:T(8,128)} copy(s32[1,4,48,4]{2,3,1,0:T(4,128)} %param.16) | data formatting | bytes 6144 | tf_op args[4]
  15.4 0.9 %copy.20 = bf16[1,4,48,4,25]{2,1,4,3,0:T(4,128)(2,1)S(1)} copy(bf16[1,4,48,4,25]{2,3,4,1,0:T(4,128)(2,1)} %param.15) | data formatting | bytes 76800 | tf_op args[3]
  16.4 0.1 reshape.36
  16.5 0.7 copy.24.stab_ref
  17.2 0.6 pad_add_fusion.where_ref
  17.8 6.3 %prep.1 = (f32[192,2560]{1,0:T(8,128)}, bf16[256,2560]{1,0:T(8,128)(2,1)}, bf16[256,2560]{1,0:T(8,128)(2,1)}, bf16[128,512]{1,0:T(8,128)(2,1)}, bf16[256,512]{1,...) custom-call(s32[2]{0:T(128)} %pad_add_fusion.where_ref, ...), custom_call_target="tpu_custom_call" | custom-call | flops 1000000000 | bytes 8000000 | tf_op jit(solution)/shard_map/prep/pallas_call | solution.py:330
  24.1 0.0 all-to-all-done.rec_ref
  24.1 0.0 copy-start
  24.1 0.7 copy-done
  24.8 9.5 %condense.1 = (bf16[256,256]{1,0:T(8,128)(2,1)}, bf16[4,192,256]{2,1,0:T(8,128)(2,1)}) custom-call(s32[2]{0:T(128)} %pad_add_fusion.where_ref, bf16[4,48,640]{2,1,0:T(8,128)(2,1)} %copy-done, f32[192,2560]{1,0:T(8,128)} %get-tuple-element.15.s_ref, bf16[256,2560]{1,0:T(8,128)(2,1)} %get-tuple-element.16.gg_ref, bf16[256,2560]{1,0:T(8,128)(2,1)} %get-tuple-element.17.qq_ref, ...), custom_call_target="tpu_custom_call" | custom-call | flops 1000000000 | bytes 8000000 | tf_op jit(solution)/shard_map/condense/pallas_call | solution.py:361
  34.3 1.6 %reshape.40 = bf16[128,2,256]{2,1,0:T(2,128)(2,1)} reshape(bf16[256,256]{1,0:T(8,128)(2,1)} %get-tuple-element.25) | data formatting | bytes 262144 | tf_op jit(solution)/shard_map/reshape | solution.py:379
  35.9 17.9 %all-to-all-start.1 = ((bf16[128,2,256]{2,1,0:T(2,128)(2,1)}), bf16[128,2,256]{2,1,0:T(2,128)(2,1)S(1)}, u32[]{:S(2)}, u32[]{:S(2)}) async-start(bf16[128,2,256]{2,1,0:T(2,128)(2,1)} %reshape.40), calls=%async_computation.1 | async-start | bytes 262144 | tf_op jit(solution)/shard_map/all_to_all | solution.py:378
  53.8 2.4 %local.1.loc_ref = f32[384,256]{1,0:T(8,128)} custom-call(bf16[4,384,192]{2,1,0:T(8,128)(2,1)} %get-tuple-element.26.hot_ref, bf16[4,192,256]{2,1,0:T(8,128)(2,1)} %get-tuple-element.27.con_ref), custom_call_target="tpu_custom_call" | custom-call | flops 300000000 | bytes 2000000 | tf_op jit(solution)/shard_map/local/pallas_call | solution.py:381
  56.2 9.9 %all-to-all-done.1 = bf16[128,2,256]{2,1,0:T(2,128)(2,1)S(1)} async-done(((bf16[128,2,256]{2,1,0:T(2,128)(2,1)}), bf16[128,2,256]{2,1,0:T(2,128)(2,1)S(1)}, u32[]{:S(2)}, u32[]{:S(2)}) %all-to-all-start.1) | async-done | bytes 131104 | tf_op jit(solution)/shard_map/all_to_all | solution.py:378
  66.1 0.7 reshape.41.got_ref
  66.8 2.1 %place.1 = bf16[4,96,256]{2,1,0:T(8,128)(2,1)} custom-call(bf16[256,256]{1,0:T(8,128)(2,1)} %reshape.41.got_ref, f32[384,256]{1,0:T(8,128)} %local.1.loc_ref), custom_call_target="tpu_custom_call" | custom-call | flops 100000000 | bytes 1000000 | tf_op jit(solution)/shard_map/place/pallas_call | solution.py:389
  68.9 9.2 %all_to_all.15.got_ref = bf16[4,96,256]{2,1,0:T(8,128)(2,1)} all-to-all(bf16[4,96,256]{2,1,0:T(8,128)(2,1)} %place.1), channel_id=1, replica_groups=mesh['section'=4,'elem'=128] {'section'}, dimensions={0} | all-to-all | bytes 393216 | tf_op jit(solution)/shard_map/all_to_all | solution.py:397
  78.1 1.7 %total.1 = (f32[3,96,50]{2,1,0:T(8,128)}, f32[3,96,50]{2,1,0:T(8,128)}) custom-call(bf16[4,96,256]{2,1,0:T(8,128)(2,1)} %all_to_all.15.got_ref), custom_call_target="tpu_custom_call" | custom-call | flops 1000000 | bytes 1000000 | tf_op jit(solution)/shard_map/total/pallas_call | solution.py:399
  79.8 1.7 %copy.27 = f32[3,96,50]{1,2,0:T(8,128)} copy(f32[3,96,50]{2,1,0:T(8,128)} %get-tuple-element.30) | data formatting | bytes 115200 | tf_op jit(solution)/shard_map/total/pallas_call | solution.py:399
  81.5 1.7 %copy.28 = f32[3,96,50]{1,2,0:T(8,128)} copy(f32[3,96,50]{2,1,0:T(8,128)} %get-tuple-element.31) | data formatting | bytes 115200 | tf_op jit(solution)/shard_map/total/pallas_call | solution.py:399
  (1 shorter events, 0.0 us)
Async XLA Ops:
  5.9 18.2 %all-to-all-start = ((bf16[4,48,640]{2,1,0:T(8,128)(2,1)}), bf16[4,48,640]{2,1,0:T(8,128)(2,1)S(1)}, u32[]{:S(2)}, u32[]{:S(2)}) async-start(bf16[4,48,640]{2,1,0:T(8,128)(2,1)} %pack.1), calls=%async_computation | async-start | bytes 491520 | tf_op jit(solution)/shard_map/all_to_all | solution.py:328
  24.1 0.7 copy-start
  35.9 30.1 %all-to-all-start.1 = ((bf16[128,2,256]{2,1,0:T(2,128)(2,1)}), bf16[128,2,256]{2,1,0:T(2,128)(2,1)S(1)}, u32[]{:S(2)}, u32[]{:S(2)}) async-start(bf16[128,2,256]{2,1,0:T(2,128)(2,1)} %reshape.40), calls=%async_computation.1 | async-start | bytes 262144 | tf_op jit(solution)/shard_map/all_to_all | solution.py:378

commit v2 on v1

v2 whole, which is shorter than its diff:
```python
import jax
import jax.numpy as jnp
import numpy as np
from jax import lax
from jax.experimental import pallas as pl
from jax.experimental.pallas import tpu as pltpu
from jax.sharding import PartitionSpec as P

TI = (
    (4.325579890063155, 0.33919925181580984, 0.5417705399358749),
    (-4.178718591551905, -0.32768282076106237, 0.47662355450055044),
    (-0.5028726349457868, 2.571926949855605, -0.5960392048282249),
)
VARS, MODES, FN, NI, NF = 5, 20, 10, 100, 50
ELEMS, COLE, GRP, COLS, FDEV = 48, 192, 64, 128, 96
SLOTS = 4 * FDEV
W = 512
UW = VARS * W
CH = 3200
BF, F32, I32 = jnp.bfloat16, jnp.float32, jnp.int32
VMEM = pl.BlockSpec(memory_space=pltpu.VMEM)


def code_tables():
    cols = np.full((16, UW), -1, np.int32)
    for u in range(VARS):
        for k in range(4):
            for o in range(2):
                for n in range(FN):
                    for v in range(VARS):
                        lane = u * W + k * 128 + o * 64 + n * VARS + v
                        cols[0, lane] = (v * 5 + u) * 4 + k
                        cols[1, lane] = k * 5 + u
                        cols[2, lane] = o * FN + n
                        cols[3, lane] = n * 4 + k
                        cols[4, lane] = u * 2 + o
                        cols[5, lane] = v if o == 0 else -1
                        cols[7, lane] = o
                        cols[8, lane] = k * 64 + n * VARS + v if o == 0 else -1
    lanes = np.arange(UW) % 128
    cols[6] = np.where(cols[0] < 0, lanes, (lanes // 64) * 64 + (lanes % 64) % 5)
    rows = np.full((256, 128), -1, np.int32)
    for i in range(256):
        if i % 64 < NF:
            rows[i, 0] = (i // 64) * 5 + i % 64 % 5
            rows[i, 1] = i % 64 // 5
    for x in range(2):
        for i in range(NI):
            rows[x * 128 + i, 2] = (i % 5) * 2 + x
            rows[x * 128 + i, 3] = i // 5
            rows[x * 128 + i, 4] = i % 5
    lane = np.arange(CH)
    tiles = np.zeros((8, CH), np.int32)
    tiles[0] = lane % NI
    tiles[1] = lane // NI
    spread = (np.arange(128)[:, None] == lane[None, :] % NI).astype(np.float32)
    return cols, rows, tiles, spread


COL_CODES, ROW_CODES, TILE_CODES, TILE_SPREAD = code_tables()


def dot(a, b):
    return lax.dot_general(a, b, (((1,), (0,)), ((), ())), preferred_element_type=F32)


def dot_t(a, b):
    return lax.dot_general(a, b, (((1,), (1,)), ((), ())), preferred_element_type=F32)


def iota(shape, dim):
    return lax.broadcasted_iota(I32, shape, dim)


def onehot(cond):
    return jnp.where(cond, 1.0, 0.0).astype(BF)


def split(x):
    hi = x.astype(BF)
    return hi, (x - hi.astype(F32)).astype(BF)


def pack_kernel(inner_ref, face_ref, trace_ref, out_ref, mix_ref):
    out_ref[...] = jnp.zeros(out_ref.shape, BF)
    mix_ref[...] = jnp.zeros(mix_ref.shape, BF)

    def place(g, lane, piece):
        cut = slice(lane, lane + piece.shape[1])
        if g == 0:
            out_ref[0, :, cut] = piece
        else:
            mix_ref[g - 1, :, cut] = piece

    for ref, lane in ((inner_ref, 0), (face_ref, 128), (trace_ref, 384)):
        vals = [ref[t].astype(F32) for t in range(3)]
        for g in range(3):
            mixed = TI[g][0] * vals[0] + TI[g][1] * vals[1] + TI[g][2] * vals[2]
            if lane == 0:
                place(g, 0, mixed.astype(BF))
            else:
                for k in range(4):
                    place(g, lane + 64 * k, mixed[:, k, :].astype(BF))
    row = iota((ELEMS, ELEMS), 0)
    pick = onehot(iota((ELEMS, ELEMS), 1) == 3 * (row & 15) + (row >> 4))
    for g in range(2):
        moved = dot(pick, mix_ref[g]).astype(BF)
        for t in range(3):
            out_ref[1 + t, 16 * g : 16 * g + 16, :] = moved[16 * t : 16 * t + 16]


def prep_kernel(
    stab_ref, orient_ref, faces_ref, lift_ref, mass_ref, cols_ref, rows_ref,
    s_ref, gg_ref, qq_ref, lm_ref, p0_ref, idx_ref, ab_ref, turned_ref, out_hot_ref,
):
    section = lax.axis_index("section")
    column = lax.axis_index("elem")
    row = iota((COLE, ELEMS), 0)
    third = section - 1
    target = jnp.where(
        section == 0, row, jnp.where(row < GRP, 48 * (row >> 4) + 3 * (row & 15) + third, -1)
    )
    face = faces_ref[...]
    block = ((face >> 5) * 43691) >> 17
    owner = block & (COLS - 1)
    slot = (block >> 7) * FDEV + face - block * FDEV
    away = owner != column
    fields = [jnp.where(away, owner + 1, 0), jnp.where(away, 0, 1), slot >> 5, slot & 31]
    fields = [field.astype(F32) for field in fields]
    stab = jnp.zeros((COLE, 100), F32)
    orient = jnp.zeros((COLE, 40), F32)
    codes = jnp.zeros((COLE, 16), F32)
    turned = jnp.zeros((16, COLE), F32)
    for s in range(4):
        pick = onehot(target == iota((COLE, ELEMS), 1) + ELEMS * s)
        stab = stab + dot_t(pick, stab_ref[s].astype(F32).reshape(100, ELEMS).astype(BF))
        orient = orient + dot_t(pick, orient_ref[s].astype(F32).reshape(40, ELEMS).astype(BF))
        field = jnp.concatenate([f[s] for f in fields], axis=0).astype(BF)
        codes = codes + dot_t(pick, field)
        turned = turned + dot_t(field, pick)
    ab_ref[...] = codes
    turned_ref[...] = turned
    stab = stab.astype(BF)
    spread_kn = onehot(iota((40, UW), 0) == cols_ref[3:4, :])
    for u in range(VARS):
        cut = slice(u * W, (u + 1) * W)
        expand = onehot(iota((100, W), 0) == cols_ref[0:1, cut])
        s_ref[:, cut] = dot(stab, expand).astype(BF)
    nodes = dot(orient.astype(BF), spread_kn[:, :W])
    idx_ref[...] = (VARS * nodes).astype(I32) + cols_ref[6:7, :W]
    pick_j = onehot(rows_ref[:, 1:2] == iota((256, FN), 1))
    eye = jnp.where(iota((FN, FN), 0) == iota((FN, FN), 1), 1.0, 0.0)
    mass = jnp.concatenate([eye, mass_ref[...].astype(F32)], axis=0).astype(BF)
    mass = dot_t(pick_j, mass).astype(BF)
    pick_m = onehot(rows_ref[:, 3:4] == iota((256, MODES), 1))
    lift = jnp.concatenate([lift_ref[n].astype(F32) for n in range(FN)], axis=0).astype(BF)
    lift = dot_t(pick_m, lift).astype(BF)
    for u in range(VARS):
        cut = slice(u * W, (u + 1) * W)
        full = dot(mass, onehot(iota((2 * FN, W), 0) == cols_ref[2:3, cut]))
        gg_ref[:, cut] = jnp.where(rows_ref[:, 0:1] == cols_ref[1:2, cut], full, 0.0).astype(BF)
        full = dot(lift, spread_kn[:, cut])
        qq_ref[:, cut] = jnp.where(rows_ref[:, 2:3] == cols_ref[4:5, cut], full, 0.0).astype(BF)
        if u == 0:
            keep = rows_ref[:128, 4:5] == cols_ref[5:6, cut]
            keep = keep & (cols_ref[5:6, cut] >= 0)
            lm_ref[...] = jnp.where(keep, full[:128], 0.0).astype(BF)
    p0_ref[...] = onehot(iota((256, W), 0) == cols_ref[8:9, :W])
    before = onehot(iota((COLE, COLE), 0) < iota((COLE, COLE), 1))
    count = jnp.zeros((COLS, 1), F32)
    own_iota = iota((COLS, COLE), 0) + 1
    for k in range(4):
        own = turned[k : k + 1, :].astype(I32)
        hot = own_iota == own
        hot_f = jnp.where(hot, 1.0, 0.0)
        rank = dot(hot_f.astype(BF), before) + count
        count = count + jnp.sum(hot_f, axis=1, keepdims=True)
        rank = jnp.sum(jnp.where(hot, rank, 0.0), axis=0, keepdims=True).astype(I32)
        key = jnp.where(own > 0, 2 * (own - 1) + rank, -1)
        out_hot_ref[k] = onehot(iota((2 * COLS, COLE), 0) == key)


def main_kernel(
    rec_ref, ab_ref, tiles_ref, cols_ref,
    s_hbm, gg_hbm, lm_hbm, tile_hbm, qq_hbm, p0_hbm, idx_hbm, hot_hbm, factor_ref,
    pay_ref, con_ref,
    s_ref, gg_ref, lm_ref, tile_ref, qq_ref, p0_ref, idx_ref, hot_ref, fac_ref, sol_ref, bd_ref,
    sem_ref, load_ref,
):
    section = lax.axis_index("section")
    pairs = (
        (gg_hbm, gg_ref), (s_hbm, s_ref), (lm_hbm, lm_ref), (tile_hbm, tile_ref), (qq_hbm, qq_ref),
        (p0_hbm, p0_ref), (idx_hbm, idx_ref), (hot_hbm, hot_ref),
    )

    def load(i):
        return pltpu.make_async_copy(pairs[i][0], pairs[i][1], load_ref.at[i])

    for i in range(4):
        load(i).start()

    def spread(x):
        total = x.shape[0]
        for j in range(5):
            cut = slice(640 * j, 640 * j + 640)
            keep = (iota((total, 640), 0) & 31) == tiles_ref[1:2, cut]
            bd_ref[:total, cut] = jnp.where(keep, dot(x, tile_ref[:, cut]), 0.0).astype(BF)

    def fetch(c):
        cut = pl.ds(c * CH, CH)
        return pltpu.make_async_copy(factor_ref.at[:, cut], fac_ref.at[:, cut], sem_ref.at[c])

    def finish(x_in, number, parts, solve):
        total = number * parts

        def s_of(u):
            s = s_ref[:number, u * W : (u + 1) * W].astype(F32)
            return jnp.concatenate([s] * parts, axis=0) if parts > 1 else s

        trace = x_in[:, 384:640]
        value = jnp.zeros((total, W), F32)
        load(0).wait()
        load(1).wait()
        for u in range(VARS):
            value = value + s_of(u) * dot(trace, gg_ref[:, u * W : (u + 1) * W])
        hi, lo = split(value)
        load(2).wait()
        lifted = (dot_t(hi, lm_ref[...]) + dot_t(lo, lm_ref[...])).astype(BF)
        sol_ref[...] = jnp.zeros(sol_ref.shape, F32)
        load(3).wait()
        solve(x_in[:, :128], lifted)
        hi, lo = split(sol_ref[:total, :])
        for i in range(4, 8):
            load(i).wait()
        base = jnp.where(cols_ref[7:8, :W] == 1, value, 0.0) + dot(x_in[:, 128:384], p0_ref[...])
        for u in range(VARS):
            cut = slice(u * W, (u + 1) * W)
            base = base - s_of(u) * (dot(hi, qq_ref[:, cut]) + dot(lo, qq_ref[:, cut]))
        con_ref[...] = jnp.zeros(con_ref.shape, BF)
        lane = iota((number, 128), 1)
        pay = [jnp.zeros((2 * COLS, 128), F32) for _ in range(parts)]
        for k in range(4):
            index = idx_ref[:number, 128 * k : 128 * k + 128]
            for c in range(parts):
                piece = base[c * number : (c + 1) * number, 128 * k : 128 * k + 128]
                piece = jnp.take_along_axis(piece, index, axis=1, mode="promise_in_bounds")
                if c == 0:
                    piece = jnp.where(lane == NF, ab_ref[:number, 8 + k : 9 + k], piece)
                    piece = jnp.where(lane == NF + 1, ab_ref[:number, 12 + k : 13 + k], piece)
                piece = piece.astype(BF)
                con_ref[k, :number, 128 * c : 128 * c + 128] = piece
                pay[c] = pay[c] + dot(hot_ref[k, :, :number], piece)
        if parts == 1:
            pay = pay + [jnp.zeros((2 * COLS, 128), F32)]
        pay = jnp.concatenate(pay, axis=1)
        pay_ref[...] = pay.reshape(COLS, 2, 256).astype(BF)

    @pl.when(section == 0)
    def _():
        for c in range(6):
            fetch(c).start()
        for i in range(4, 8):
            load(i).start()
        x_in = jnp.concatenate([rec_ref[s] for s in range(4)], axis=0)

        def solve(inner, lifted):
            cuts = [slice(32 * c, 32 * c + 32) for c in range(6)]
            spread(jnp.concatenate([a[cut] for cut in cuts for a in (inner, lifted)], axis=0))
            for c, cut in enumerate(cuts):
                fetch(c).wait()
                y = dot_t(bd_ref[64 * c : 64 * c + 64, :], fac_ref[:, c * CH : (c + 1) * CH])
                sol_ref[cut, 0:NI] = y[:32]
                sol_ref[cut, 128 : 128 + NI] = y[32:]

        finish(x_in, COLE, 1, solve)

    @pl.when(section != 0)
    def _():
        for c in range(4):
            fetch(c).start()
        for i in range(4, 8):
            load(i).start()
        x_in = jnp.concatenate(
            [rec_ref[s, 16 * g : 16 * g + 16] for g in range(2) for s in range(4)], axis=0
        )

        def solve(inner, lifted):
            res = [slice(32 * c, 32 * c + 32) for c in range(2)]
            ims = [slice(GRP + 32 * c, GRP + 32 * c + 32) for c in range(2)]
            spread(
                jnp.concatenate(
                    [a[cut] for c in range(2) for cut in (res[c], ims[c]) for a in (inner, lifted)],
                    axis=0,
                )
            )
            for c, (re, im) in enumerate(zip(res, ims)):
                x = bd_ref[128 * c : 128 * c + 128, :]
                fetch(c).wait()
                a = dot_t(x, fac_ref[:, c * CH : (c + 1) * CH])
                fetch(2 + c).wait()
                b = dot_t(x, fac_ref[:, (2 + c) * CH : (3 + c) * CH])
                real = a[:64] - b[64:]
                imag = b[:64] + a[64:]
                sol_ref[re, 0:NI] = real[:32]
                sol_ref[re, 128 : 128 + NI] = real[32:]
                sol_ref[im, 0:NI] = imag[:32]
                sol_ref[im, 128 : 128 + NI] = imag[32:]

        finish(x_in, GRP, 2, solve)


def local_kernel(turned_ref, con_ref, out_ref):
    total = jnp.zeros(out_ref.shape, F32)
    for k in range(4):
        slots = 32.0 * turned_ref[8 + k : 9 + k, :] + turned_ref[12 + k : 13 + k, :]
        slots = jnp.where(turned_ref[4 + k : 5 + k, :] > 0.5, slots, -1.0).astype(I32)
        total = total + dot(onehot(iota((SLOTS, COLE), 0) == slots), con_ref[k])
    out_ref[...] = total


def place_kernel(got_ref, loc_ref, out_ref):
    got = got_ref[...].astype(F32).reshape(2 * COLS, 256).astype(BF)
    lane = iota((8, 128), 1)
    weights = jnp.where(lane == NF, 32.0, jnp.where(lane == NF + 1, 1.0, 0.0)).astype(BF)
    slot = dot_t(weights, got[:, :128])[0:1].astype(I32)
    hot = onehot(iota((SLOTS, 2 * COLS), 0) == slot)
    total = loc_ref[...] + dot(hot, got)
    for s in range(4):
        out_ref[s] = total[FDEV * s : FDEV * s + FDEV].astype(BF)


def sum_kernel(got_ref, res_ref, schur_ref):
    three = got_ref[1].astype(F32) + got_ref[2].astype(F32) + got_ref[3].astype(F32)
    for g, part in enumerate((got_ref[0, :, :128].astype(F32), three[:, :128], three[:, 128:])):
        part = part.T
        res_ref[g] = part[:NF]
        schur_ref[g] = part[64 : 64 + NF]


def shape(dims, kind):
    return jax.ShapeDtypeStruct(dims, kind)


def hold(x):
    return pltpu.with_memory_space_constraint(x, pltpu.VMEM)


def cost(flops, nbytes):
    return pl.CostEstimate(flops=flops, bytes_accessed=nbytes, transcendentals=0)


def on_device(
    interior_res, face_res, trace_vals, stabil, element_faces, orient, lift_matrix, face_matrix, factors
):
    params = pltpu.CompilerParams(vmem_limit_bytes=59 * 2**20)
    send = pl.pallas_call(
        pack_kernel,
        name="pack",
        out_shape=shape((4, ELEMS, 640), BF),
        in_specs=[VMEM] * 3,
        out_specs=VMEM,
        scratch_shapes=[pltpu.VMEM((2, ELEMS, 640), BF)],
        compiler_params=params,
        cost_estimate=cost(10**8, 10**6),
    )(
        interior_res.reshape(3, ELEMS, NI),
        face_res.reshape(3, ELEMS, 4, NF),
        trace_vals.reshape(3, ELEMS, 4, NF),
    )
    received = hold(lax.all_to_all(send, "section", split_axis=0, concat_axis=0, tiled=True))
    cols, rows, tiles = jnp.asarray(COL_CODES), jnp.asarray(ROW_CODES), jnp.asarray(TILE_CODES)
    s_all, gg, qq, lm, p0, idx, ab, turned, out_hot = pl.pallas_call(
        prep_kernel,
        name="prep",
        out_shape=(
            shape((COLE, UW), BF),
            shape((256, UW), BF),
            shape((256, UW), BF),
            shape((128, W), BF),
            shape((256, W), BF),
            shape((COLE, W), I32),
            shape((COLE, 16), F32),
            shape((16, COLE), F32),
            shape((4, 2 * COLS, COLE), BF),
        ),
        in_specs=[VMEM] * 7,
        out_specs=[VMEM] * 9,
        compiler_params=params,
        cost_estimate=cost(10**9, 8 * 10**6),
    )(
        stabil[0].transpose(0, 3, 2, 1),
        orient[0].transpose(0, 3, 2, 1),
        element_faces[0].transpose(0, 2, 1),
        lift_matrix.transpose(2, 0, 1),
        face_matrix,
        cols,
        rows,
    )
    payload, contrib = pl.pallas_call(
        main_kernel,
        name="condense",
        out_shape=(shape((COLS, 2, 256), BF), shape((4, COLE, 256), BF)),
        in_specs=[VMEM] * 4 + [pl.BlockSpec(memory_space=pltpu.HBM)] * 9,
        out_specs=[VMEM] * 2,
        scratch_shapes=[
            pltpu.VMEM((COLE, UW), BF),
            pltpu.VMEM((256, UW), BF),
            pltpu.VMEM((128, W), BF),
            pltpu.VMEM((128, CH), BF),
            pltpu.VMEM((256, UW), BF),
            pltpu.VMEM((256, W), BF),
            pltpu.VMEM((COLE, W), I32),
            pltpu.VMEM((4, 2 * COLS, COLE), BF),
            pltpu.VMEM((NI, COLE * NI), BF),
            pltpu.VMEM((COLE, 256), F32),
            pltpu.VMEM((2 * COLE, CH), BF),
            pltpu.SemaphoreType.DMA((6,)),
            pltpu.SemaphoreType.DMA((8,)),
        ],
        compiler_params=params,
        cost_estimate=cost(10**9, 8 * 10**6),
    )(
        received, ab, tiles, cols,
        s_all, gg, lm, jnp.asarray(TILE_SPREAD, BF), qq, p0, idx, out_hot, factors.reshape(NI, COLE * NI),
    )
    got = hold(lax.all_to_all(payload, "elem", split_axis=0, concat_axis=0, tiled=True))
    local = pl.pallas_call(
        local_kernel,
        name="local",
        out_shape=shape((SLOTS, 256), F32),
        in_specs=[VMEM] * 2,
        out_specs=VMEM,
        compiler_params=params,
        cost_estimate=cost(3 * 10**8, 2 * 10**6),
    )(turned, contrib)
    partial = pl.pallas_call(
        place_kernel,
        name="place",
        out_shape=shape((4, FDEV, 256), BF),
        in_specs=[VMEM] * 2,
        out_specs=VMEM,
        compiler_params=params,
        cost_estimate=cost(10**8, 10**6),
    )(got, local)
    parts = hold(lax.all_to_all(partial, "section", split_axis=0, concat_axis=0, tiled=True))
    outs = pl.pallas_call(
        sum_kernel,
        name="total",
        out_shape=(shape((3, NF, FDEV), F32), shape((3, NF, FDEV), F32)),
        in_specs=[VMEM],
        out_specs=[VMEM] * 2,
        compiler_params=params,
        cost_estimate=cost(10**6, 10**6),
    )(parts)
    return tuple(out.transpose(0, 2, 1) for out in outs)


def solution(mesh):
    return jax.shard_map(
        on_device,
        mesh=mesh,
        in_specs=(
            P(None, "elem", "section", None, None),
            P(None, "elem", "section", None, None, None),
            P(None, "elem", "section", None, None, None),
            P("elem", None, None, None, None),
            P("elem", None, None, None),
            P("elem", None, None, None, None),
            P(),
            P(),
            P("section", "elem", None, None),
        ),
        out_specs=(P(None, ("section", "elem"), None), P(None, ("section", "elem"), None)),
        check_vma=False,
    )
```

time: 83.9 us -> 65.9 us (0.79)
  local copies, waits for them, and re-layouts: 15.3 us -> 0 us
  Pallas kernels: 23.7 us -> 22 us
  other arithmetic: 1.51 us -> 0 us
  starting transfers between devices: 22.7 us -> 23.9 us
    reshape x8 -> x0, local copies, waits for them, and re-layouts: 8.09 us -> none  [the longest x1 1.7 us: on_device(): face_res.reshape(3, ELEMS, 4 * NF)]
    pallas_call x2 -> x0, local copies, waits for them, and re-layouts: 3.31 us -> none  [on_device(): pl.pallas_call(sum_kernel, name='total', out_shape=(shape((3, FDEV, NF),...]
    unnamed x4 -> x0, local copies, waits for them, and re-layouts: 3.09 us -> none
    pallas_call x3, Pallas kernels: 17.4 us -> 15.4 us  [the longest x1 9.51 us: on_device(): pl.pallas_call(main_kernel, name='condense', out_shape=(shape((COLS, 2, 2...]
    all_to_all x1, starting transfers between devices: 17.9 us -> 19 us  [on_device(): lax.all_to_all(payload, 'elem', split_axis=0, concat_axis=0, tiled=True)]
    convert_element_type x1 -> x0, other arithmetic: 0.9 us -> none  [on_device(): orient.reshape(COLE, 40).astype(BF)]
  transfers between devices with their start and end apart: 2 -> 2, of which waited for: 1 -> 2; matrix products, arithmetic and copies ran while one was open for 9% -> 0% of each run, Pallas kernels for 10% -> 11%
where the time goes in v2:
time: 65.9 us; the launch traced here: 65.5 us
  starting transfers between devices  23.9 us (36%)
  Pallas kernels  22 us (33%)
  waiting for transfers between devices  10.4 us (16%)
  blocking collectives  8.51 us (13%)
    all_to_all x1, starting transfers between devices, on_device(): lax.all_to_all(payload, 'elem', split_axis=0, concat_axis=0, tiled=True)  19 us
    all_to_all x1, waiting for transfers between devices, on_device(): lax.all_to_all(payload, 'elem', split_axis=0, concat_axis=0, tiled=True)  10.1 us
    pallas_call x1, Pallas kernels, on_device(): pl.pallas_call(main_kernel, name='condense', out_shape=(shape((COLS, 2, 2...  9.51 us
    all_to_all x1, blocking collectives, on_device(): lax.all_to_all(partial, 'section', split_axis=0, concat_axis=0, tiled=True)  8.51 us
    pallas_call x1, Pallas kernels, on_device(): pl.pallas_call(prep_kernel, name='prep', out_shape=(shape((COLE, UW), BF)...  5.13 us
    all_to_all x1, starting transfers between devices, on_device(): lax.all_to_all(send, 'section', split_axis=0, concat_axis=0, tiled=True)  4.83 us
    pallas_call x1, Pallas kernels, on_device(): pl.pallas_call(pack_kernel, name='pack', out_shape=shape((4, ELEMS, 640),...  2.43 us
    pallas_call x1, Pallas kernels, on_device(): pl.pallas_call(local_kernel, name='local', out_shape=shape((SLOTS, 256),...  2.13 us
  transfers between devices with their start and end apart: 2, of which 2 were waited for; matrix products, arithmetic and copies ran while one was open for 0% of the time, Pallas kernels for 11%

profile of v2, /device:TPU:1, one launch (start us, length us, event | category | flops | bytes accessed | tf_op | source)
XLA Modules:
  0.0 65.5 jit_solution(6523812599045919724)
XLA Ops:
  0.6 2.4 %pack.1 = bf16[4,48,640]{2,1,0:T(8,128)(2,1)} custom-call(bf16[3,48,100]{2,1,0:T(8,128)(2,1)} %bitcast.19, bf16[3,48,4,50]{3,2,1,0:T(4,128)(2,1)} %bitcast.17, bf16[3,48,4,50]{3,2,1,0:T(4,128)(2,1)} %bitcast.18), custom_call_target="tpu_custom_call" | custom-call | flops 100000000 | bytes 1000000 | tf_op jit(solution)/shard_map/pack/pallas_call | solution.py:356
  3.1 4.8 %all-to-all-start = ((bf16[4,48,640]{2,1,0:T(8,128)(2,1)}), bf16[4,48,640]{2,1,0:T(8,128)(2,1)S(1)}, u32[]{:S(2)}, u32[]{:S(2)}) async-start(bf16[4,48,640]{2,1,0:T(8,128)(2,1)} %pack.1), calls=%async_computation | async-start | bytes 491520 | tf_op jit(solution)/shard_map/all_to_all | solution.py:370
  7.9 5.1 %prep.1 = (bf16[192,2560]{1,0:T(8,128)(2,1)}, bf16[256,2560]{1,0:T(8,128)(2,1)}, bf16[256,2560]{1,0:T(8,128)(2,1)}, bf16[128,512]{1,0:T(8,128)(2,1)}, bf16[256,5...) custom-call(bf16[4,25,4,48]{3,2,1,0:T(4,128)(2,1)} %bitcast.20, ...), custom_call_target="tpu_custom_call" | custom-call | flops 1000000000 | bytes 8000000 | tf_op jit(solution)/shard_map/prep/pallas_call | solution.py:372
  13.0 0.3 all-to-all-done.rec_ref
  13.3 9.5 %condense.1 = (bf16[128,2,256]{2,1,0:T(2,128)(2,1)}, bf16[4,192,256]{2,1,0:T(8,128)(2,1)}) custom-call(bf16[4,48,640]{2,1,0:T(8,128)(2,1)S(1)} %all-to-all-done.rec_ref, f32[192,16]{1,0:T(8,128)} %get-tuple-element.15.ab_ref, s32[8,3200]{1,0:T(8,128)} %constant.10.clone.tiles_ref, s32[16,2560]{1,0:T(8,128)} %constant.8.clone.cols_ref, ...), custom_call_target="tpu_custom_call" | custom-call | flops 1000000000 | bytes 8000000 | tf_op jit(solution)/shard_map/condense/pallas_call | solution.py:399
  22.8 19.0 %all-to-all-start.1 = ((bf16[128,2,256]{2,1,0:T(2,128)(2,1)}), bf16[128,2,256]{2,1,0:T(2,128)(2,1)S(1)}, u32[]{:S(2)}, u32[]{:S(2)}) async-start(bf16[128,2,256]{2,1,0:T(2,128)(2,1)} %get-tuple-element.23), calls=%async_computation.1 | async-start | bytes 262144 | tf_op jit(solution)/shard_map/all_to_all | solution.py:426
  41.9 2.1 %local.1.loc_ref = f32[384,256]{1,0:T(8,128)} custom-call(f32[16,192]{1,0:T(8,128)} %get-tuple-element.24.turned_ref, bf16[4,192,256]{2,1,0:T(8,128)(2,1)} %get-tuple-element.25.con_ref), custom_call_target="tpu_custom_call" | custom-call | flops 300000000 | bytes 2000000 | tf_op jit(solution)/shard_map/local/pallas_call | solution.py:427
  44.0 10.1 %all-to-all-done.1.got_ref = bf16[128,2,256]{2,1,0:T(2,128)(2,1)S(1)} async-done(((bf16[128,2,256]{2,1,0:T(2,128)(2,1)}), bf16[128,2,256]{2,1,0:T(2,128)(2,1)S(1)}, u32[]{:S(2)}, u32[]{:S(2)}) %all-to-all-start.1) | async-done | bytes 131104 | tf_op jit(solution)/shard_map/all_to_all | solution.py:426
  54.1 2.0 %place.1 = bf16[4,96,256]{2,1,0:T(8,128)(2,1)} custom-call(bf16[128,2,256]{2,1,0:T(2,128)(2,1)S(1)} %all-to-all-done.1.got_ref, f32[384,256]{1,0:T(8,128)} %local.1.loc_ref), custom_call_target="tpu_custom_call" | custom-call | flops 100000000 | bytes 1000000 | tf_op jit(solution)/shard_map/place/pallas_call | solution.py:436
  56.2 8.5 %all_to_all.15.got_ref = bf16[4,96,256]{2,1,0:T(8,128)(2,1)S(1)} all-to-all(bf16[4,96,256]{2,1,0:T(8,128)(2,1)} %place.1), channel_id=1, replica_groups=mesh['section'=4,'elem'=128] {'section'}, dimensions={0} | all-to-all | bytes 393216 | tf_op jit(solution)/shard_map/all_to_all | solution.py:445
  64.7 0.8 %total.1 = (f32[3,50,96]{2,1,0:T(8,128)}, f32[3,50,96]{2,1,0:T(8,128)}) custom-call(bf16[4,96,256]{2,1,0:T(8,128)(2,1)S(1)} %all_to_all.15.got_ref), custom_call_target="tpu_custom_call" | custom-call | flops 1000000 | bytes 1000000 | tf_op jit(solution)/shard_map/total/pallas_call | solution.py:446
Async XLA Ops:
  3.1 10.3 %all-to-all-start = ((bf16[4,48,640]{2,1,0:T(8,128)(2,1)}), bf16[4,48,640]{2,1,0:T(8,128)(2,1)S(1)}, u32[]{:S(2)}, u32[]{:S(2)}) async-start(bf16[4,48,640]{2,1,0:T(8,128)(2,1)} %pack.1), calls=%async_computation | async-start | bytes 491520 | tf_op jit(solution)/shard_map/all_to_all | solution.py:370
  22.8 31.3 %all-to-all-start.1 = ((bf16[128,2,256]{2,1,0:T(2,128)(2,1)}), bf16[128,2,256]{2,1,0:T(2,128)(2,1)S(1)}, u32[]{:S(2)}, u32[]{:S(2)}) async-start(bf16[128,2,256]{2,1,0:T(2,128)(2,1)} %get-tuple-element.23), calls=%async_computation.1 | async-start | bytes 262144 | tf_op jit(solution)/shard_map/all_to_all | solution.py:426

commit v3 on v2

--- a/solution.py
+++ b/solution.py
@@ -50,14 +50,11 @@
             rows[x * 128 + i, 3] = i // 5
             rows[x * 128 + i, 4] = i % 5
     lane = np.arange(CH)
-    tiles = np.zeros((8, CH), np.int32)
-    tiles[0] = lane % NI
-    tiles[1] = lane // NI
     spread = (np.arange(128)[:, None] == lane[None, :] % NI).astype(np.float32)
-    return cols, rows, tiles, spread
-
-
-COL_CODES, ROW_CODES, TILE_CODES, TILE_SPREAD = code_tables()
+    return cols, rows, spread
+
+
+COL_CODES, ROW_CODES, TILE_SPREAD = code_tables()
 
 
 def dot(a, b):
@@ -181,16 +178,17 @@
 
 
 def main_kernel(
-    rec_ref, ab_ref, tiles_ref, cols_ref,
-    s_hbm, gg_hbm, lm_hbm, tile_hbm, qq_hbm, p0_hbm, idx_hbm, hot_hbm, factor_ref,
+    rec_ref, s_hbm, gg_hbm, lm_hbm, tile_hbm, qq_hbm, p0_hbm, idx_hbm, hot_hbm, ab_hbm, factor_ref,
     pay_ref, con_ref,
-    s_ref, gg_ref, lm_ref, tile_ref, qq_ref, p0_ref, idx_ref, hot_ref, fac_ref, sol_ref, bd_ref,
-    sem_ref, load_ref,
+    s_ref, gg_ref, lm_ref, tile_ref, qq_ref, p0_ref, idx_ref, hot_ref, ab_ref, fac_ref,
+    sol_ref, bd_ref, sem_ref, load_ref,
 ):
     section = lax.axis_index("section")
     pairs = (
-        (gg_hbm, gg_ref), (s_hbm, s_ref), (lm_hbm, lm_ref), (tile_hbm, tile_ref), (qq_hbm, qq_ref),
-        (p0_hbm, p0_ref), (idx_hbm, idx_ref), (hot_hbm, hot_ref),
+        (gg_hbm, gg_ref), (s_hbm, s_ref), (lm_hbm, lm_ref), (tile_hbm, tile_ref),
+        (qq_hbm, qq_ref.at[0:256]),
+        (p0_hbm, p0_ref), (idx_hbm, idx_ref), (hot_hbm, hot_ref), (ab_hbm, ab_ref),
+        (qq_hbm, qq_ref.at[256:512]),
     )
 
     def load(i):
@@ -199,12 +197,18 @@
     for i in range(4):
         load(i).start()
 
-    def spread(x):
-        total = x.shape[0]
-        for j in range(5):
-            cut = slice(640 * j, 640 * j + 640)
-            keep = (iota((total, 640), 0) & 31) == tiles_ref[1:2, cut]
-            bd_ref[:total, cut] = jnp.where(keep, dot(x, tile_ref[:, cut]), 0.0).astype(BF)
+    def spread(sides, chunks):
+        part = 8 * len(sides)
+        for e in range(4):
+            low, high = 800 * e // 128 * 128, -(-800 * (e + 1) // 128) * 128
+            at = [slice(32 * c + 8 * e, 32 * c + 8 * e + 8) for c in range(chunks)]
+            x = jnp.concatenate([side[cut] for cut in at for side in sides], axis=0).astype(BF)
+            size = (x.shape[0], high - low)
+            keep = (iota(size, 0) & 7) + 8 * e == ((iota(size, 1) + low) * 5243) >> 19
+            x = jnp.where(keep, dot(x, tile_ref[:, low:high]), 0.0).astype(BF)
+            for c in range(chunks):
+                row = 4 * part * c + part * e
+                bd_ref[row : row + part, low:high] = x[part * c : part * c + part]
 
     def fetch(c):
         cut = pl.ds(c * CH, CH)
@@ -218,6 +222,8 @@
             return jnp.concatenate([s] * parts, axis=0) if parts > 1 else s
 
         trace = x_in[:, 384:640]
+        bd_ref[: 2 * total, :] = jnp.zeros((2 * total, CH), BF)
+        sol_ref[...] = jnp.zeros(sol_ref.shape, F32)
         value = jnp.zeros((total, W), F32)
         load(0).wait()
         load(1).wait()
@@ -226,16 +232,16 @@
         hi, lo = split(value)
         load(2).wait()
         lifted = (dot_t(hi, lm_ref[...]) + dot_t(lo, lm_ref[...])).astype(BF)
-        sol_ref[...] = jnp.zeros(sol_ref.shape, F32)
+        lifted = lifted.astype(F32)
         load(3).wait()
-        solve(x_in[:, :128], lifted)
-        hi, lo = split(sol_ref[:total, :])
-        for i in range(4, 8):
+        solve(x_in[:, :128].astype(F32), lifted)
+        both = jnp.concatenate(split(sol_ref[:total, :]), axis=1)
+        for i in range(4, 10):
             load(i).wait()
-        base = jnp.where(cols_ref[7:8, :W] == 1, value, 0.0) + dot(x_in[:, 128:384], p0_ref[...])
+        base = jnp.where((iota((total, W), 1) & 64) != 0, value, 0.0) + dot(x_in[:, 128:384], p0_ref[...])
         for u in range(VARS):
             cut = slice(u * W, (u + 1) * W)
-            base = base - s_of(u) * (dot(hi, qq_ref[:, cut]) + dot(lo, qq_ref[:, cut]))
+            base = base - s_of(u) * dot(both, qq_ref[:, cut])
         con_ref[...] = jnp.zeros(con_ref.shape, BF)
         lane = iota((number, 128), 1)
         pay = [jnp.zeros((2 * COLS, 128), F32) for _ in range(parts)]
@@ -259,18 +265,19 @@
     def _():
         for c in range(6):
             fetch(c).start()
-        for i in range(4, 8):
+        for i in range(4, 10):
             load(i).start()
         x_in = jnp.concatenate([rec_ref[s] for s in range(4)], axis=0)
 
         def solve(inner, lifted):
-            cuts = [slice(32 * c, 32 * c + 32) for c in range(6)]
-            spread(jnp.concatenate([a[cut] for cut in cuts for a in (inner, lifted)], axis=0))
-            for c, cut in enumerate(cuts):
+            spread([inner, lifted], 6)
+            for c in range(6):
                 fetch(c).wait()
                 y = dot_t(bd_ref[64 * c : 64 * c + 64, :], fac_ref[:, c * CH : (c + 1) * CH])
-                sol_ref[cut, 0:NI] = y[:32]
-                sol_ref[cut, 128 : 128 + NI] = y[32:]
+                for e in range(4):
+                    cut = slice(32 * c + 8 * e, 32 * c + 8 * e + 8)
+                    sol_ref[cut, 0:NI] = y[16 * e : 16 * e + 8]
+                    sol_ref[cut, 128 : 128 + NI] = y[16 * e + 8 : 16 * e + 16]
 
         finish(x_in, COLE, 1, solve)
 
@@ -278,33 +285,27 @@
     def _():
         for c in range(4):
             fetch(c).start()
-        for i in range(4, 8):
+        for i in range(4, 10):
             load(i).start()
         x_in = jnp.concatenate(
             [rec_ref[s, 16 * g : 16 * g + 16] for g in range(2) for s in range(4)], axis=0
         )
 
         def solve(inner, lifted):
-            res = [slice(32 * c, 32 * c + 32) for c in range(2)]
-            ims = [slice(GRP + 32 * c, GRP + 32 * c + 32) for c in range(2)]
-            spread(
-                jnp.concatenate(
-                    [a[cut] for c in range(2) for cut in (res[c], ims[c]) for a in (inner, lifted)],
-                    axis=0,
-                )
-            )
-            for c, (re, im) in enumerate(zip(res, ims)):
+            spread([inner[:GRP], lifted[:GRP], inner[GRP:], lifted[GRP:]], 2)
+            for c in range(2):
                 x = bd_ref[128 * c : 128 * c + 128, :]
                 fetch(c).wait()
                 a = dot_t(x, fac_ref[:, c * CH : (c + 1) * CH])
                 fetch(2 + c).wait()
                 b = dot_t(x, fac_ref[:, (2 + c) * CH : (3 + c) * CH])
-                real = a[:64] - b[64:]
-                imag = b[:64] + a[64:]
-                sol_ref[re, 0:NI] = real[:32]
-                sol_ref[re, 128 : 128 + NI] = real[32:]
-                sol_ref[im, 0:NI] = imag[:32]
-                sol_ref[im, 128 : 128 + NI] = imag[32:]
+                for e in range(4):
+                    re, im = slice(32 * e, 32 * e + 16), slice(32 * e + 16, 32 * e + 32)
+                    both = (a[re] - b[im], b[re] + a[im])
+                    for g in range(2):
+                        row = GRP * g + 32 * c + 8 * e
+                        sol_ref[row : row + 8, 0:NI] = both[g][:8]
+                        sol_ref[row : row + 8, 128 : 128 + NI] = both[g][8:]
 
         finish(x_in, GRP, 2, solve)
 
@@ -318,13 +319,17 @@
     out_ref[...] = total
 
 
-def place_kernel(got_ref, loc_ref, out_ref):
+def place_kernel(got_ref, loc_hbm, out_ref, loc_ref, sem_ref):
+    load = pltpu.make_async_copy(loc_hbm, loc_ref, sem_ref)
+    load.start()
     got = got_ref[...].astype(F32).reshape(2 * COLS, 256).astype(BF)
     lane = iota((8, 128), 1)
     weights = jnp.where(lane == NF, 32.0, jnp.where(lane == NF + 1, 1.0, 0.0)).astype(BF)
     slot = dot_t(weights, got[:, :128])[0:1].astype(I32)
     hot = onehot(iota((SLOTS, 2 * COLS), 0) == slot)
-    total = loc_ref[...] + dot(hot, got)
+    total = dot(hot, got)
+    load.wait()
+    total = total + loc_ref[...]
     for s in range(4):
         out_ref[s] = total[FDEV * s : FDEV * s + FDEV].astype(BF)
 
@@ -339,6 +344,10 @@
 
 def shape(dims, kind):
     return jax.ShapeDtypeStruct(dims, kind)
+
+
+def on_chip(dims, kind):
+    return pltpu.VMEM(dims, kind)
 
 
 def hold(x):
@@ -368,7 +377,7 @@
         trace_vals.reshape(3, ELEMS, 4, NF),
     )
     received = hold(lax.all_to_all(send, "section", split_axis=0, concat_axis=0, tiled=True))
-    cols, rows, tiles = jnp.asarray(COL_CODES), jnp.asarray(ROW_CODES), jnp.asarray(TILE_CODES)
+    cols, rows = jnp.asarray(COL_CODES), jnp.asarray(ROW_CODES)
     s_all, gg, qq, lm, p0, idx, ab, turned, out_hot = pl.pallas_call(
         prep_kernel,
         name="prep",
@@ -400,28 +409,28 @@
         main_kernel,
         name="condense",
         out_shape=(shape((COLS, 2, 256), BF), shape((4, COLE, 256), BF)),
-        in_specs=[VMEM] * 4 + [pl.BlockSpec(memory_space=pltpu.HBM)] * 9,
+        in_specs=[VMEM] + [pl.BlockSpec(memory_space=pltpu.HBM)] * 10,
         out_specs=[VMEM] * 2,
         scratch_shapes=[
             pltpu.VMEM((COLE, UW), BF),
             pltpu.VMEM((256, UW), BF),
             pltpu.VMEM((128, W), BF),
             pltpu.VMEM((128, CH), BF),
-            pltpu.VMEM((256, UW), BF),
+            pltpu.VMEM((512, UW), BF),
             pltpu.VMEM((256, W), BF),
             pltpu.VMEM((COLE, W), I32),
             pltpu.VMEM((4, 2 * COLS, COLE), BF),
+            pltpu.VMEM((COLE, 16), F32),
             pltpu.VMEM((NI, COLE * NI), BF),
             pltpu.VMEM((COLE, 256), F32),
             pltpu.VMEM((2 * COLE, CH), BF),
             pltpu.SemaphoreType.DMA((6,)),
-            pltpu.SemaphoreType.DMA((8,)),
+            pltpu.SemaphoreType.DMA((10,)),
         ],
         compiler_params=params,
         cost_estimate=cost(10**9, 8 * 10**6),
     )(
-        received, ab, tiles, cols,
-        s_all, gg, lm, jnp.asarray(TILE_SPREAD, BF), qq, p0, idx, out_hot, factors.reshape(NI, COLE * NI),
+        received, s_all, gg, lm, jnp.asarray(TILE_SPREAD, BF), qq, p0, idx, out_hot, ab, factors.reshape(NI, COLE * NI),
     )
     got = hold(lax.all_to_all(payload, "elem", split_axis=0, concat_axis=0, tiled=True))
     local = pl.pallas_call(
@@ -436,9 +445,10 @@
     partial = pl.pallas_call(
         place_kernel,
         name="place",
-        out_shape=shape((4, FDEV, 256), BF),
-        in_specs=[VMEM] * 2,
+        out_shape=on_chip((4, FDEV, 256), BF),
+        in_specs=[VMEM, pl.BlockSpec(memory_space=pltpu.HBM)],
         out_specs=VMEM,
+        scratch_shapes=[pltpu.VMEM((SLOTS, 256), F32), pltpu.SemaphoreType.DMA(())],
         compiler_params=params,
         cost_estimate=cost(10**8, 10**6),
     )(got, local)

time: 65.9 us -> 62.7 us (0.951)
  Pallas kernels: 22 us -> 19.8 us
  blocking collectives: 8.51 us -> 7.54 us
    pallas_call x1, Pallas kernels: 9.51 us -> 8.11 us  [on_device(): pl.pallas_call(main_kernel, name='condense', out_shape=(shape((COLS, 2, 2...]
    all_to_all x1, blocking collectives: 8.51 us -> 7.54 us  [on_device(): lax.all_to_all(partial, 'section', split_axis=0, concat_axis=0, tiled=True)]
    pallas_call x1, Pallas kernels: 2.04 us -> 1.25 us  [on_device(): pl.pallas_call(place_kernel, name='place', out_shape=on_chip((4, FDEV, 25...]
  transfers between devices with their start and end apart: 2 -> 2, of which waited for: 2 -> 2; matrix products, arithmetic and copies ran while one was open for 0% -> 0% of each run, Pallas kernels for 11% -> 12%
where the time goes in v3:
time: 62.7 us; the launch traced here: 62.3 us
  starting transfers between devices  23.9 us (38%)
  Pallas kernels  19.8 us (32%)
  waiting for transfers between devices  10.4 us (17%)
  blocking collectives  7.54 us (12%)
  between operations  0.66 us (1%)
    all_to_all x1, starting transfers between devices, on_device(): lax.all_to_all(payload, 'elem', split_axis=0, concat_axis=0, tiled=True)  19 us
    all_to_all x1, waiting for transfers between devices, on_device(): lax.all_to_all(payload, 'elem', split_axis=0, concat_axis=0, tiled=True)  10.1 us
    pallas_call x1, Pallas kernels, on_device(): pl.pallas_call(main_kernel, name='condense', out_shape=(shape((COLS, 2, 2...  8.11 us
    all_to_all x1, blocking collectives, on_device(): lax.all_to_all(partial, 'section', split_axis=0, concat_axis=0, tiled=True)  7.54 us
    pallas_call x1, Pallas kernels, on_device(): pl.pallas_call(prep_kernel, name='prep', out_shape=(shape((COLE, UW), BF)...  5.13 us
    all_to_all x1, starting transfers between devices, on_device(): lax.all_to_all(send, 'section', split_axis=0, concat_axis=0, tiled=True)  4.83 us
    pallas_call x1, Pallas kernels, on_device(): pl.pallas_call(pack_kernel, name='pack', out_shape=shape((4, ELEMS, 640),...  2.43 us
    pallas_call x1, Pallas kernels, on_device(): pl.pallas_call(local_kernel, name='local', out_shape=shape((SLOTS, 256),...  2.13 us
  transfers between devices with their start and end apart: 2, of which 2 were waited for; matrix products, arithmetic and copies ran while one was open for 0% of the time, Pallas kernels for 12%

profile of v3, /device:TPU:1, one launch (start us, length us, event | category | flops | bytes accessed | tf_op | source)
XLA Modules:
  0.0 62.3 jit_solution(600213436864702719)
XLA Ops:
  0.6 2.4 %pack.1 = bf16[4,48,640]{2,1,0:T(8,128)(2,1)} custom-call(bf16[3,48,100]{2,1,0:T(8,128)(2,1)} %bitcast.19, bf16[3,48,4,50]{3,2,1,0:T(4,128)(2,1)} %bitcast.17, bf16[3,48,4,50]{3,2,1,0:T(4,128)(2,1)} %bitcast.18), custom_call_target="tpu_custom_call" | custom-call | flops 100000000 | bytes 1000000 | tf_op jit(solution)/shard_map/pack/pallas_call | solution.py:365
  3.1 4.8 %all-to-all-start = ((bf16[4,48,640]{2,1,0:T(8,128)(2,1)}), bf16[4,48,640]{2,1,0:T(8,128)(2,1)S(1)}, u32[]{:S(2)}, u32[]{:S(2)}) async-start(bf16[4,48,640]{2,1,0:T(8,128)(2,1)} %pack.1), calls=%async_computation | async-start | bytes 491520 | tf_op jit(solution)/shard_map/all_to_all | solution.py:379
  7.9 5.1 %prep.1 = (bf16[192,2560]{1,0:T(8,128)(2,1)}, bf16[256,2560]{1,0:T(8,128)(2,1)}, bf16[256,2560]{1,0:T(8,128)(2,1)}, bf16[128,512]{1,0:T(8,128)(2,1)}, bf16[256,5...) custom-call(bf16[4,25,4,48]{3,2,1,0:T(4,128)(2,1)} %bitcast.20, ...), custom_call_target="tpu_custom_call" | custom-call | flops 1000000000 | bytes 8000000 | tf_op jit(solution)/shard_map/prep/pallas_call | solution.py:381
  13.0 0.3 all-to-all-done.rec_ref
  13.3 8.1 %condense.1 = (bf16[128,2,256]{2,1,0:T(2,128)(2,1)}, bf16[4,192,256]{2,1,0:T(8,128)(2,1)}) custom-call(bf16[4,48,640]{2,1,0:T(8,128)(2,1)S(1)} %all-to-all-done.rec_ref, bf16[192,2560]{1,0:T(8,128)(2,1)} %get-tuple-element.15.s_hbm, bf16[256,2560]{1,0:T(8,128)(2,1)} %get-tuple-element.16.gg_hbm, bf16[128,512]{1,0:T(8,128)(2,1)} %get-tuple-element.17.lm_hbm, ...), custom_call_target="tpu_custom_call" | custom-call | flops 1000000000 | bytes 8000000 | tf_op jit(solution)/shard_map/condense/pallas_call | solution.py:408
  21.4 19.0 %all-to-all-start.1 = ((bf16[128,2,256]{2,1,0:T(2,128)(2,1)}), bf16[128,2,256]{2,1,0:T(2,128)(2,1)S(1)}, u32[]{:S(2)}, u32[]{:S(2)}) async-start(bf16[128,2,256]{2,1,0:T(2,128)(2,1)} %get-tuple-element.23), calls=%async_computation.1 | async-start | bytes 262144 | tf_op jit(solution)/shard_map/all_to_all | solution.py:435
  40.5 2.1 %local.1.loc_hbm = f32[384,256]{1,0:T(8,128)} custom-call(f32[16,192]{1,0:T(8,128)} %get-tuple-element.24.turned_ref, bf16[4,192,256]{2,1,0:T(8,128)(2,1)} %get-tuple-element.25.con_ref), custom_call_target="tpu_custom_call" | custom-call | flops 300000000 | bytes 2000000 | tf_op jit(solution)/shard_map/local/pallas_call | solution.py:436
  42.6 10.1 %all-to-all-done.1.got_ref = bf16[128,2,256]{2,1,0:T(2,128)(2,1)S(1)} async-done(((bf16[128,2,256]{2,1,0:T(2,128)(2,1)}), bf16[128,2,256]{2,1,0:T(2,128)(2,1)S(1)}, u32[]{:S(2)}, u32[]{:S(2)}) %all-to-all-start.1) | async-done | bytes 131104 | tf_op jit(solution)/shard_map/all_to_all | solution.py:435
  52.7 1.3 %place.1 = bf16[4,96,256]{2,1,0:T(8,128)(2,1)S(1)} custom-call(bf16[128,2,256]{2,1,0:T(2,128)(2,1)S(1)} %all-to-all-done.1.got_ref, f32[384,256]{1,0:T(8,128)} %local.1.loc_hbm), custom_call_target="tpu_custom_call" | custom-call | flops 100000000 | bytes 1000000 | tf_op jit(solution)/shard_map/place/pallas_call | solution.py:445
  54.0 7.5 %all_to_all.15.got_ref = bf16[4,96,256]{2,1,0:T(8,128)(2,1)S(1)} all-to-all(bf16[4,96,256]{2,1,0:T(8,128)(2,1)S(1)} %place.1), channel_id=1, replica_groups=mesh['section'=4,'elem'=128] {'section'}, dimensions={0} | all-to-all | bytes 393216 | tf_op jit(solution)/shard_map/all_to_all | solution.py:455
  61.6 0.8 %total.1 = (f32[3,50,96]{2,1,0:T(8,128)}, f32[3,50,96]{2,1,0:T(8,128)}) custom-call(bf16[4,96,256]{2,1,0:T(8,128)(2,1)S(1)} %all_to_all.15.got_ref), custom_call_target="tpu_custom_call" | custom-call | flops 1000000 | bytes 1000000 | tf_op jit(solution)/shard_map/total/pallas_call | solution.py:456
Async XLA Ops:
  3.1 10.3 %all-to-all-start = ((bf16[4,48,640]{2,1,0:T(8,128)(2,1)}), bf16[4,48,640]{2,1,0:T(8,128)(2,1)S(1)}, u32[]{:S(2)}, u32[]{:S(2)}) async-start(bf16[4,48,640]{2,1,0:T(8,128)(2,1)} %pack.1), calls=%async_computation | async-start | bytes 491520 | tf_op jit(solution)/shard_map/all_to_all | solution.py:379
  21.4 31.3 %all-to-all-start.1 = ((bf16[128,2,256]{2,1,0:T(2,128)(2,1)}), bf16[128,2,256]{2,1,0:T(2,128)(2,1)S(1)}, u32[]{:S(2)}, u32[]{:S(2)}) async-start(bf16[128,2,256]{2,1,0:T(2,128)(2,1)} %get-tuple-element.23), calls=%async_computation.1 | async-start | bytes 262144 | tf_op jit(solution)/shard_map/all_to_all | solution.py:435

commit v4 on v3

--- a/solution.py
+++ b/solution.py
@@ -78,7 +78,7 @@
     return hi, (x - hi.astype(F32)).astype(BF)
 
 
-def pack_kernel(inner_ref, face_ref, trace_ref, out_ref, mix_ref):
+def pack_kernel(inner_ref, face_ref, trace_ref, out_ref, mix_ref, row_ref):
     out_ref[...] = jnp.zeros(out_ref.shape, BF)
     mix_ref[...] = jnp.zeros(mix_ref.shape, BF)
 
@@ -91,13 +91,18 @@
 
     for ref, lane in ((inner_ref, 0), (face_ref, 128), (trace_ref, 384)):
         vals = [ref[t].astype(F32) for t in range(3)]
+        if lane > 0:
+            vals = [val.reshape(COLE, NF) for val in vals]
         for g in range(3):
             mixed = TI[g][0] * vals[0] + TI[g][1] * vals[1] + TI[g][2] * vals[2]
             if lane == 0:
                 place(g, 0, mixed.astype(BF))
             else:
+                at = g if lane == 128 else 3 + g
+                row_ref[at] = mixed
                 for k in range(4):
-                    place(g, lane + 64 * k, mixed[:, k, :].astype(BF))
+                    piece = row_ref[at, pl.ds(k, ELEMS, stride=4), :]
+                    place(g, lane + 64 * k, piece.astype(BF))
     row = iota((ELEMS, ELEMS), 0)
     pick = onehot(iota((ELEMS, ELEMS), 1) == 3 * (row & 15) + (row >> 4))
     for g in range(2):
@@ -138,12 +143,12 @@
     ab_ref[...] = codes
     turned_ref[...] = turned
     stab = stab.astype(BF)
-    spread_kn = onehot(iota((40, UW), 0) == cols_ref[3:4, :])
+    spread_kn = onehot(iota((40, W), 0) == cols_ref[3:4, :W])
     for u in range(VARS):
         cut = slice(u * W, (u + 1) * W)
         expand = onehot(iota((100, W), 0) == cols_ref[0:1, cut])
         s_ref[:, cut] = dot(stab, expand).astype(BF)
-    nodes = dot(orient.astype(BF), spread_kn[:, :W])
+    nodes = dot(orient.astype(BF), spread_kn)
     idx_ref[...] = (VARS * nodes).astype(I32) + cols_ref[6:7, :W]
     pick_j = onehot(rows_ref[:, 1:2] == iota((256, FN), 1))
     eye = jnp.where(iota((FN, FN), 0) == iota((FN, FN), 1), 1.0, 0.0)
@@ -152,11 +157,11 @@
     pick_m = onehot(rows_ref[:, 3:4] == iota((256, MODES), 1))
     lift = jnp.concatenate([lift_ref[n].astype(F32) for n in range(FN)], axis=0).astype(BF)
     lift = dot_t(pick_m, lift).astype(BF)
+    massed = dot(mass, onehot(iota((2 * FN, W), 0) == cols_ref[2:3, :W]))
+    full = dot(lift, spread_kn)
     for u in range(VARS):
         cut = slice(u * W, (u + 1) * W)
-        full = dot(mass, onehot(iota((2 * FN, W), 0) == cols_ref[2:3, cut]))
-        gg_ref[:, cut] = jnp.where(rows_ref[:, 0:1] == cols_ref[1:2, cut], full, 0.0).astype(BF)
-        full = dot(lift, spread_kn[:, cut])
+        gg_ref[:, cut] = jnp.where(rows_ref[:, 0:1] == cols_ref[1:2, cut], massed, 0.0).astype(BF)
         qq_ref[:, cut] = jnp.where(rows_ref[:, 2:3] == cols_ref[4:5, cut], full, 0.0).astype(BF)
         if u == 0:
             keep = rows_ref[:128, 4:5] == cols_ref[5:6, cut]
@@ -368,7 +373,7 @@
         out_shape=shape((4, ELEMS, 640), BF),
         in_specs=[VMEM] * 3,
         out_specs=VMEM,
-        scratch_shapes=[pltpu.VMEM((2, ELEMS, 640), BF)],
+        scratch_shapes=[pltpu.VMEM((2, ELEMS, 640), BF), pltpu.VMEM((6, COLE, NF), F32)],
         compiler_params=params,
         cost_estimate=cost(10**8, 10**6),
     )(

time: 62.7 us -> 62.6 us (level)
  Pallas kernels: 19.8 us -> 18.9 us
  waiting for transfers between devices: 10.4 us -> 11.2 us
    all_to_all x1, waiting for transfers between devices: 0.31 us -> 1.06 us  [on_device(): lax.all_to_all(send, 'section', split_axis=0, concat_axis=0, tiled=True)]
    pallas_call x1, Pallas kernels: 5.13 us -> 4.38 us  [on_device(): pl.pallas_call(prep_kernel, name='prep', out_shape=(shape((COLE, UW), BF)...]
  transfers between devices with their start and end apart: 2 -> 2, of which waited for: 2 -> 2; matrix products, arithmetic and copies ran while one was open for 0% -> 0% of each run, Pallas kernels for 12% -> 10%
where the time goes in v4:
time: 62.6 us; the launch traced here: 62.2 us
  starting transfers between devices  23.9 us (38%)
  Pallas kernels  18.9 us (30%)
  waiting for transfers between devices  11.2 us (18%)
  blocking collectives  7.54 us (12%)
  between operations  0.66 us (1%)
    all_to_all x1, starting transfers between devices, on_device(): lax.all_to_all(payload, 'elem', split_axis=0, concat_axis=0, tiled=True)  19 us
    all_to_all x1, waiting for transfers between devices, on_device(): lax.all_to_all(payload, 'elem', split_axis=0, concat_axis=0, tiled=True)  10.1 us
    pallas_call x1, Pallas kernels, on_device(): pl.pallas_call(main_kernel, name='condense', out_shape=(shape((COLS, 2, 2...  8.11 us
    all_to_all x1, blocking collectives, on_device(): lax.all_to_all(partial, 'section', split_axis=0, concat_axis=0, tiled=True)  7.54 us
    all_to_all x1, starting transfers between devices, on_device(): lax.all_to_all(send, 'section', split_axis=0, concat_axis=0, tiled=True)  4.83 us
    pallas_call x1, Pallas kernels, on_device(): pl.pallas_call(prep_kernel, name='prep', out_shape=(shape((COLE, UW), BF)...  4.38 us
    pallas_call x1, Pallas kernels, on_device(): pl.pallas_call(pack_kernel, name='pack', out_shape=shape((4, ELEMS, 640),...  2.28 us
    pallas_call x1, Pallas kernels, on_device(): pl.pallas_call(local_kernel, name='local', out_shape=shape((SLOTS, 256),...  2.13 us
  transfers between devices with their start and end apart: 2, of which 2 were waited for; matrix products, arithmetic and copies ran while one was open for 0% of the time, Pallas kernels for 10%

profile of v4, /device:TPU:1, one launch (start us, length us, event | category | flops | bytes accessed | tf_op | source)
XLA Modules:
  0.0 62.2 jit_solution(10742132046445573721)
XLA Ops:
  0.6 2.3 %pack.1 = bf16[4,48,640]{2,1,0:T(8,128)(2,1)} custom-call(bf16[3,48,100]{2,1,0:T(8,128)(2,1)} %bitcast.19, bf16[3,48,4,50]{3,2,1,0:T(4,128)(2,1)} %bitcast.17, bf16[3,48,4,50]{3,2,1,0:T(4,128)(2,1)} %bitcast.18), custom_call_target="tpu_custom_call" | custom-call | flops 100000000 | bytes 1000000 | tf_op jit(solution)/shard_map/pack/pallas_call | solution.py:370
  2.9 4.8 %all-to-all-start = ((bf16[4,48,640]{2,1,0:T(8,128)(2,1)}), bf16[4,48,640]{2,1,0:T(8,128)(2,1)S(1)}, u32[]{:S(2)}, u32[]{:S(2)}) async-start(bf16[4,48,640]{2,1,0:T(8,128)(2,1)} %pack.1), calls=%async_computation | async-start | bytes 491520 | tf_op jit(solution)/shard_map/all_to_all | solution.py:384
  7.7 4.4 %prep.1 = (bf16[192,2560]{1,0:T(8,128)(2,1)}, bf16[256,2560]{1,0:T(8,128)(2,1)}, bf16[256,2560]{1,0:T(8,128)(2,1)}, bf16[128,512]{1,0:T(8,128)(2,1)}, bf16[256,5...) custom-call(bf16[4,25,4,48]{3,2,1,0:T(4,128)(2,1)} %bitcast.20, ...), custom_call_target="tpu_custom_call" | custom-call | flops 1000000000 | bytes 8000000 | tf_op jit(solution)/shard_map/prep/pallas_call | solution.py:386
  12.1 1.1 %all-to-all-done.rec_ref = bf16[4,48,640]{2,1,0:T(8,128)(2,1)S(1)} async-done(((bf16[4,48,640]{2,1,0:T(8,128)(2,1)}), bf16[4,48,640]{2,1,0:T(8,128)(2,1)S(1)}, u32[]{:S(2)}, u32[]{:S(2)}) %all-to-all-start) | async-done | bytes 245792 | tf_op jit(solution)/shard_map/all_to_all | solution.py:384
  13.2 8.1 %condense.1 = (bf16[128,2,256]{2,1,0:T(2,128)(2,1)}, bf16[4,192,256]{2,1,0:T(8,128)(2,1)}) custom-call(bf16[4,48,640]{2,1,0:T(8,128)(2,1)S(1)} %all-to-all-done.rec_ref, bf16[192,2560]{1,0:T(8,128)(2,1)} %get-tuple-element.15.s_hbm, bf16[256,2560]{1,0:T(8,128)(2,1)} %get-tuple-element.16.gg_hbm, bf16[128,512]{1,0:T(8,128)(2,1)} %get-tuple-element.17.lm_hbm, ...), custom_call_target="tpu_custom_call" | custom-call | flops 1000000000 | bytes 8000000 | tf_op jit(solution)/shard_map/condense/pallas_call | solution.py:413
  21.3 19.0 %all-to-all-start.1 = ((bf16[128,2,256]{2,1,0:T(2,128)(2,1)}), bf16[128,2,256]{2,1,0:T(2,128)(2,1)S(1)}, u32[]{:S(2)}, u32[]{:S(2)}) async-start(bf16[128,2,256]{2,1,0:T(2,128)(2,1)} %get-tuple-element.23), calls=%async_computation.1 | async-start | bytes 262144 | tf_op jit(solution)/shard_map/all_to_all | solution.py:440
  40.3 2.1 %local.1.loc_hbm = f32[384,256]{1,0:T(8,128)} custom-call(f32[16,192]{1,0:T(8,128)} %get-tuple-element.24.turned_ref, bf16[4,192,256]{2,1,0:T(8,128)(2,1)} %get-tuple-element.25.con_ref), custom_call_target="tpu_custom_call" | custom-call | flops 300000000 | bytes 2000000 | tf_op jit(solution)/shard_map/local/pallas_call | solution.py:441
  42.5 10.1 %all-to-all-done.1.got_ref = bf16[128,2,256]{2,1,0:T(2,128)(2,1)S(1)} async-done(((bf16[128,2,256]{2,1,0:T(2,128)(2,1)}), bf16[128,2,256]{2,1,0:T(2,128)(2,1)S(1)}, u32[]{:S(2)}, u32[]{:S(2)}) %all-to-all-start.1) | async-done | bytes 131104 | tf_op jit(solution)/shard_map/all_to_all | solution.py:440
  52.6 1.3 %place.1 = bf16[4,96,256]{2,1,0:T(8,128)(2,1)S(1)} custom-call(bf16[128,2,256]{2,1,0:T(2,128)(2,1)S(1)} %all-to-all-done.1.got_ref, f32[384,256]{1,0:T(8,128)} %local.1.loc_hbm), custom_call_target="tpu_custom_call" | custom-call | flops 100000000 | bytes 1000000 | tf_op jit(solution)/shard_map/place/pallas_call | solution.py:450
  53.9 7.5 %all_to_all.15.got_ref = bf16[4,96,256]{2,1,0:T(8,128)(2,1)S(1)} all-to-all(bf16[4,96,256]{2,1,0:T(8,128)(2,1)S(1)} %place.1), channel_id=1, replica_groups=mesh['section'=4,'elem'=128] {'section'}, dimensions={0} | all-to-all | bytes 393216 | tf_op jit(solution)/shard_map/all_to_all | solution.py:460
  61.4 0.8 %total.1 = (f32[3,50,96]{2,1,0:T(8,128)}, f32[3,50,96]{2,1,0:T(8,128)}) custom-call(bf16[4,96,256]{2,1,0:T(8,128)(2,1)S(1)} %all_to_all.15.got_ref), custom_call_target="tpu_custom_call" | custom-call | flops 1000000 | bytes 1000000 | tf_op jit(solution)/shard_map/total/pallas_call | solution.py:461
Async XLA Ops:
  2.9 10.3 %all-to-all-start = ((bf16[4,48,640]{2,1,0:T(8,128)(2,1)}), bf16[4,48,640]{2,1,0:T(8,128)(2,1)S(1)}, u32[]{:S(2)}, u32[]{:S(2)}) async-start(bf16[4,48,640]{2,1,0:T(8,128)(2,1)} %pack.1), calls=%async_computation | async-start | bytes 491520 | tf_op jit(solution)/shard_map/all_to_all | solution.py:384
  21.3 31.3 %all-to-all-start.1 = ((bf16[128,2,256]{2,1,0:T(2,128)(2,1)}), bf16[128,2,256]{2,1,0:T(2,128)(2,1)S(1)}, u32[]{:S(2)}, u32[]{:S(2)}) async-start(bf16[128,2,256]{2,1,0:T(2,128)(2,1)} %get-tuple-element.23), calls=%async_computation.1 | async-start | bytes 262144 | tf_op jit(solution)/shard_map/all_to_all | solution.py:440
